TPU v7x, 32 devices: a whole 2x2x4 slice. The times are simulated.
32 devices in a mesh: grp: 2 (over y), vec: 4 (over z), wlk: 4 (over x, core).
Axes of the slice: x: 2, y: 2, z: 4, core: 2. Of those that a mesh axis runs over, the one named last changes fastest.
Arguments:
- cholesky: bfloat16 [48, 64, 512], P(('grp', 'vec')), parts along dimension 0
- orbitals: float32 [32, 64, 512], P(('grp', 'vec', 'wlk')), parts along dimension 0, may hold values from -6 to 6
- log_weights: float32 [32], P(('grp', 'vec', 'wlk')), parts along dimension 0, may hold values from -6 to 6
- parents: int32 [32], P(('grp', 'vec', 'wlk')), parts along dimension 0, may hold values from 0 to 3
- propagator: float32 [1024, 512], P('grp'), parts along dimension 0
Outputs:
- new_orbitals: float32 [32, 64, 512], P(('grp', 'vec', 'wlk')), parts along dimension 0
- new_log_weights: float32 [32], P(('grp', 'vec', 'wlk')), parts along dimension 0
There are 2 independent parts, one for each index of `grp`. A program takes and returns all parts, laid end to end along the dimension named above; each array names one. Nothing has to cross between parts.
Inputs may be any that keep to these rules, and one draw needn't show every extreme that they name: parents[w] counts within the aligned block of 4 consecutive walkers that holds w.
All inputs are finite; a program needn't handle non-finite values.
Results may differ from a plain program's by a relative error of at most 0.02.
Values may be sent and summed in bfloat16 or wider, within the bound.
A program may use at most 64 MiB of HBM per device.

v0:
```python
import functools
import math

import jax
import jax.numpy as jnp
from jax import lax
from jax.experimental import pallas as pl
from jax.experimental.pallas import tpu as pltpu
from jax.sharding import PartitionSpec as P

NS_ITERS = 2

gradient_step = 0.25
energy_step = 0.002
epsilon = 1e-06

MESH = pl.DeviceIdType.MESH
UNROLL_LIMIT = 8


def dot(a, b):
    return lax.dot_general(a, b, (((1,), (0,)), ((), ())), preferred_element_type=jnp.float32)


def dot_t(a, b):
    return lax.dot_general(a, b, (((1,), (1,)), ((), ())), preferred_element_type=jnp.float32)


def each(count, body):
    if count <= UNROLL_LIMIT:
        for j in range(count):
            body(j)
    else:
        lax.fori_loop(0, count, lambda j, c: (body(j), c)[1], 0)


def by_distance(me, n, j):
    side = lax.div(2 * me, n)
    near = me + side * (n - 1 - 2 * me)
    spot = n - 1 - j - lax.div(near + j + 1, n)
    return spot + side * (n - 1 - 2 * spot)


def by_chip(me, n, j):
    if n % 2:
        return lax.rem(me + 1 + j, n)
    step = j + 2
    core = lax.rem(me + lax.rem(step, 2) + lax.div(step, n), 2)
    return lax.rem((lax.div(me, 2) + lax.div(step, 2)) * 2 + core, n)


def kernel(
    n_vec, n_wlk, vecs,
    chol_hbm, orb_hbm, logw_hbm, par_hbm, prop_hbm,
    out_ref, outlog_ref,
    logw, par, orb, prop, propb, pop, tile, chosen, turned, shared, gsend, grecv, esend, erecv, acc, eacc,
    load_sem, c_load, c_send, c_recv, r_send, p_send, p_recv, t_send, t_recv,
    g_send, g_recv, e_send, e_recv,
):
    me = lax.axis_index("vec")
    mw = lax.axis_index("wlk")
    occ, basis = orb.shape
    slots = shared.shape[1] // occ
    scale = 1.0 / math.sqrt(vecs * n_vec)
    others, peers = n_vec - 1, n_wlk - 1

    half = n_wlk // 2
    place = lax.rem(mw, 2) * half + lax.div(mw, 2) if n_wlk % 2 == 0 else mw

    def in_slot(slot, body):
        if (slot + 1) * n_wlk <= vecs:
            body()
        else:
            pl.when(slot * n_wlk + place < vecs)(body)

    def share(slot):
        return pl.ds(pl.multiple_of((slot * n_wlk + place) * occ, occ), occ)

    def spot(slot):
        return pl.ds(slot * occ, occ)

    def own_copy(slot):
        return pltpu.make_async_copy(
            chol_hbm.at[share(slot)], shared.at[me, spot(slot)], c_load.at[slot])

    def vector_copy(slot, src, dst):
        return pltpu.make_async_remote_copy(
            src_ref=chol_hbm.at[share(slot)], dst_ref=shared.at[src, spot(slot)],
            send_sem=c_send.at[slot, dst], recv_sem=c_recv.at[slot, src],
            device_id={"vec": dst}, device_id_type=MESH)

    side = lax.div(2 * me, n_vec)
    near = me + side * (n_vec - 1 - 2 * me)
    near_end, far_end = side * (n_vec - 1), n_vec - 1 - side * (n_vec - 1)
    relayed = n_vec >= 4

    def relay_copy(slot):
        return pltpu.make_async_remote_copy(
            src_ref=shared.at[far_end, spot(slot)], dst_ref=shared.at[far_end, spot(slot)],
            send_sem=r_send.at[slot], recv_sem=c_recv.at[slot, far_end],
            device_id={"vec": near_end}, device_id_type=MESH)

    def relay():
        for slot in range(slots):
            def forward():
                vector_copy(slot, far_end, me).wait_recv()
                relay_copy(slot).start()

            in_slot(slot, forward)

    def to_peer(src_ref, dst_ref, send, recv, dst):
        return pltpu.make_async_remote_copy(
            src_ref=src_ref, dst_ref=dst_ref, send_sem=send, recv_sem=recv,
            device_id={"wlk": dst}, device_id_type=MESH)

    def walker_copy(src, dst):
        return to_peer(pop.at[src], pop.at[src], p_send.at[dst], p_recv.at[src], dst)

    def tile_copy(src, dst):
        return to_peer(tile.at[src], tile.at[src], t_send.at[dst], t_recv.at[src], dst)

    def gradient_copy(src, dst):
        return to_peer(gsend.at[dst], grecv.at[src], g_send.at[dst], g_recv.at[src], dst)

    def energy_copy(src, dst):
        return to_peer(esend.at[dst], erecv.at[src], e_send.at[dst], e_recv.at[src], dst)

    loads = [
        pltpu.make_async_copy(src, dst, load_sem.at[i])
        for i, (src, dst) in enumerate((
            (orb_hbm, orb), (par_hbm, par), (logw_hbm, logw), (prop_hbm, prop)))
    ]
    for load in loads:
        load.start()
    load_orb, load_par, load_logw, load_prop = loads

    barrier = pltpu.get_barrier_semaphore()

    def greet_vec(j):
        pl.semaphore_signal(
            barrier, inc=1, device_id={"vec": by_distance(me, n_vec, j)}, device_id_type=MESH)

    def greet_wlk(j):
        pl.semaphore_signal(
            barrier, inc=1, device_id={"wlk": by_chip(mw, n_wlk, j)}, device_id_type=MESH)

    each(others, greet_vec)
    each(peers, greet_wlk)
    for slot in range(slots):
        in_slot(slot, lambda: own_copy(slot).start())
        if (slot + 1) * n_wlk > vecs:
            @pl.when(slot * n_wlk + place >= vecs)
            def _():
                shared[:, slot * occ:(slot + 1) * occ, :] = jnp.zeros(
                    (n_vec, occ, basis), jnp.bfloat16)
    pl.semaphore_wait(barrier, others + peers)

    for slot in range(slots):
        def send_vectors():
            def send_far():
                vector_copy(slot, me, far_end).start()

            if relayed:
                pl.when(near > 0)(send_far)
            else:
                send_far()
            each(others - 1, lambda j: vector_copy(
                slot, me, by_distance(me, n_vec, j + 1)).start())

        in_slot(slot, send_vectors)
    load_orb.wait()
    pop[mw] = orb[...].astype(jnp.bfloat16)
    load_logw.wait()
    load_par.wait()
    tile[mw, 0:8] = jnp.broadcast_to(logw[...], (8, 128))
    tile[mw, 8:16] = jnp.broadcast_to(par[...], (8, 128)).astype(jnp.float32)
    each(peers, lambda j: walker_copy(mw, by_chip(mw, n_wlk, j)).start())
    each(peers, lambda j: tile_copy(mw, by_chip(mw, n_wlk, j)).start())

    load_prop.wait()
    propb[...] = prop[...].T.astype(jnp.bfloat16)
    each(peers, lambda j: tile_copy(by_chip(mw, n_wlk, j), mw).wait_recv())
    each(peers, lambda j: walker_copy(by_chip(mw, n_wlk, j), mw).wait_recv())

    def pick(parent, read):
        value = read(0)
        for m in range(1, n_wlk):
            value = jnp.where(parent == m, read(m), value)
        return value

    for k in range(n_wlk):
        parent = jnp.broadcast_to(tile[k, 8:9, 0:1], (occ, basis))
        rows = pick(parent, lambda m: pop[m].astype(jnp.float32))
        chosen[k] = rows.astype(jnp.bfloat16)
        turned[k] = rows.T.astype(jnp.bfloat16)
    chosen_log = pick(tile[mw, 8:16], lambda m: tile[m, 0:8])

    row = lax.broadcasted_iota(jnp.int32, (occ, occ), 0)
    col = lax.broadcasted_iota(jnp.int32, (occ, occ), 1)
    diagonal = row == col

    def contribution(source, finish):
        vectors = shared[source]
        order = [by_chip(mw, n_wlk, j) for j in range(peers)] + [mw]
        products = [dot(vectors, turned[k]) for k in order]
        parts = []
        for s in products:
            blocks = []
            exchange = jnp.zeros((occ, occ), jnp.float32)
            squares = jnp.zeros((1, 1), jnp.float32)
            for g in range(slots):
                sg = s[g * occ:(g + 1) * occ, :]
                on_diagonal = jnp.where(diagonal, sg, 0.0)
                tg = jnp.sum(jnp.sum(on_diagonal, axis=0, keepdims=True), axis=1, keepdims=True)
                exchange = exchange + sg * sg.T
                squares = squares + tg * tg
                blocks.append((scale * (jnp.where(diagonal, tg, 0.0) - sg)).astype(jnp.bfloat16))
            adjoint = jnp.concatenate(blocks, axis=1) if slots > 1 else blocks[0]
            total = jnp.sum(jnp.sum(exchange, axis=0, keepdims=True), axis=1, keepdims=True)
            energy = jnp.broadcast_to(0.5 * scale * (squares - total), (8, 128))
            parts.append((dot(adjoint, vectors), energy))
        for j, (gradient, energy) in enumerate(parts):
            finish(j, order[j], gradient, energy)

    def begin(j, k, gradient, energy):
        acc[k] = gradient
        eacc[k] = energy

    def add(j, k, gradient, energy):
        acc[k] += gradient
        eacc[k] += energy

    def add_and_give(j, k, gradient, energy):
        if j == peers:
            add(j, k, gradient, energy)
            return
        esend[k] = eacc[k] + energy
        energy_copy(mw, k).start()
        gsend[k] = (acc[k] + gradient).astype(jnp.bfloat16)
        gradient_copy(mw, k).start()

    for slot in range(slots):
        in_slot(slot, lambda: own_copy(slot).wait())
    contribution(me, begin)

    def await_vectors(src):
        for slot in range(slots):
            in_slot(slot, lambda: vector_copy(slot, src, me).wait_recv())

    def serve(j):
        src = by_distance(me, n_vec, others - 1 - j)
        await_vectors(src)
        contribution(src, add)

    if relayed:
        serve(0)
        pl.when(near == 1)(relay)
        each(others - 2, lambda j: serve(j + 1))
        pl.when(near != 1)(lambda: await_vectors(far_end))
    else:
        each(others - 1, serve)
        await_vectors(far_end)
    contribution(far_end, add_and_give)

    acc[mw] = chosen[mw].astype(jnp.float32) - gradient_step * acc[mw]

    def collect(j):
        src = by_chip(mw, n_wlk, peers - 1 - j)
        gradient_copy(src, mw).wait_recv()
        acc[mw] -= gradient_step * grecv[src].astype(jnp.float32)

    def collect_energy(j):
        src = by_chip(mw, n_wlk, peers - 1 - j)
        energy_copy(src, mw).wait_recv()
        eacc[mw] += erecv[src]

    each(peers, collect)
    each(peers, collect_energy)
    outlog_ref[0] = jnp.max(chosen_log - energy_step * eacc[mw])

    x = dot(acc[mw].astype(jnp.bfloat16), propb[...])
    mean_square = jnp.sum(jnp.sum(x * x, axis=0, keepdims=True), axis=1, keepdims=True)
    mean_square = mean_square / (occ * basis)
    norm = 1.0 / jnp.sqrt(mean_square + epsilon)
    for step in range(NS_ITERS):
        xb = x.astype(jnp.bfloat16)
        inter = dot_t(xb, xb) * (norm * norm / basis if step == 0 else 1.0 / basis)
        x = 0.5 * (3.0 * x - dot(inter.astype(jnp.bfloat16), xb))
        if step == 0:
            x = norm * x
    out_ref[...] = x


    def drain_vec(dst):
        for slot in range(slots):
            in_slot(slot, lambda: vector_copy(slot, me, dst).wait_send())

    def drain_relay():
        for slot in range(slots):
            in_slot(slot, lambda: relay_copy(slot).wait_send())

    def drain_wlk(j):
        dst = by_chip(mw, n_wlk, j)
        walker_copy(mw, dst).wait_send()
        tile_copy(mw, dst).wait_send()
        gradient_copy(mw, dst).wait_send()
        energy_copy(mw, dst).wait_send()

    if relayed:
        pl.when(near > 0)(lambda: drain_vec(far_end))
        pl.when(near == 1)(drain_relay)
    else:
        drain_vec(far_end)
    each(others - 1, lambda j: drain_vec(by_distance(me, n_vec, j + 1)))
    each(peers, drain_wlk)


def solution(mesh):
    n_vec, n_wlk = mesh.shape["vec"], mesh.shape["wlk"]

    def local(cholesky, orbitals, log_weights, parents, propagator):
        walkers, occ, basis = orbitals.shape
        assert walkers == 1
        vecs = cholesky.shape[0]
        slots = -(-vecs // n_wlk)
        f32, bf16 = jnp.float32, jnp.bfloat16
        dma = pltpu.SemaphoreType.DMA
        hbm = pl.BlockSpec(memory_space=pltpu.HBM)
        smem = pl.BlockSpec(memory_space=pltpu.SMEM)
        out, logs = pl.pallas_call(
            functools.partial(kernel, n_vec, n_wlk, vecs),
            out_shape=(
                pltpu.VMEM((occ, basis), f32),
                jax.ShapeDtypeStruct((1,), f32),
            ),
            in_specs=[hbm] * 5,
            out_specs=(pl.BlockSpec(memory_space=pltpu.VMEM), smem),
            scratch_shapes=[
                pltpu.VMEM((1, 1), f32),
                pltpu.VMEM((1, 1), jnp.int32),
                pltpu.VMEM((occ, basis), f32),
                pltpu.VMEM(propagator.shape, f32),
                pltpu.VMEM(propagator.shape, bf16),
                pltpu.VMEM((n_wlk, occ, basis), bf16),
                pltpu.VMEM((n_wlk, 16, 128), f32),
                pltpu.VMEM((n_wlk, occ, basis), bf16),
                pltpu.VMEM((n_wlk, basis, occ), bf16),
                pltpu.VMEM((n_vec, slots * occ, basis), bf16),
                pltpu.VMEM((n_wlk, occ, basis), bf16),
                pltpu.VMEM((n_wlk, occ, basis), bf16),
                pltpu.VMEM((n_wlk, 8, 128), f32),
                pltpu.VMEM((n_wlk, 8, 128), f32),
                pltpu.VMEM((n_wlk, occ, basis), f32),
                pltpu.VMEM((n_wlk, 8, 128), f32),
                dma((4,)),
                dma((slots,)), dma((slots, n_vec)), dma((slots, n_vec)), dma((slots,)),
            ] + [dma((n_wlk,))] * 8,
            compiler_params=pltpu.CompilerParams(
                collective_id=0, has_side_effects=True, vmem_limit_bytes=66400000),
        )(
            cholesky.reshape(vecs * occ, basis),
            orbitals.reshape(occ, basis),
            log_weights.reshape(1, 1),
            parents.reshape(1, 1),
            propagator,
        )
        return out.reshape(orbitals.shape), logs

    placed = (
        P(("grp", "vec"), None, None),
        P(("grp", "vec", "wlk"), None, None),
        P(("grp", "vec", "wlk")),
        P(("grp", "vec", "wlk")),
        P("grp", None),
    )
    return jax.shard_map(
        local,
        mesh=mesh,
        in_specs=placed,
        out_specs=(P(("grp", "vec", "wlk"), None, None), P(("grp", "vec", "wlk"))),
        check_vma=False,
    )
```

profile of v0, /device:TPU:1, one launch (start us, length us, event | category | flops | bytes accessed | tf_op | source)
XLA Modules:
  0.0 26.2 jit_solution(79893871509930314)
XLA Ops:
  1.9 21.9 %shard_map.68 = (f32[64,512]{1,0:T(8,128)S(1)}, f32[1]{0:T(128)}) custom-call(bf16[384,512]{1,0:T(8,128)(2,1)} %bitcast.8, f32[64,512]{1,0:T(8,128)} %bitcast.9, f32[1,1]{1,0:T(1,128)} %bitcast.5.logw_hbm, s32[1,1]{1,0:T(1,128)} %bitcast.6.par_hbm, f32[512,512]{1,0:T(8,128)} %prop_hbm.1), custom_call_target="tpu_custom_call" | custom-call | tf_op jit(solution)/shard_map/pallas_call | solution.py:330
  23.8 0.7 %copy.9 = f32[1,64,512]{2,1,0:T(8,128)} copy(f32[1,64,512]{2,1,0:T(8,128)S(1)} %bitcast.7) | data formatting | bytes 262144
where the time goes:
time: 26.3 us; the launch traced here: 26.2 us
  Pallas kernels  21.9 us (83%)
  between operations  3.62 us (14%)
  local copies, waits for them, and re-layouts  0.66 us (3%)
    pallas_call x1, Pallas kernels, local(): pl.pallas_call(functools.partial(kernel, n_vec, n_wlk, vecs), out_shape=(...  21.9 us
    unnamed x1, local copies, waits for them, and re-layouts  0.66 us

commit v1 on v0

v1 whole, which is shorter than its diff:
```python
import functools
import math

import jax
import jax.numpy as jnp
from jax import lax
from jax.experimental import pallas as pl
from jax.experimental.pallas import tpu as pltpu
from jax.sharding import PartitionSpec as P

NS_ITERS = 2

gradient_step = 0.25
energy_step = 0.002
epsilon = 1e-06

MESH = pl.DeviceIdType.MESH
UNROLL_LIMIT = 8
PIECES = 3
EXTRA = 16


def dot(a, b):
    return lax.dot_general(a, b, (((1,), (0,)), ((), ())), preferred_element_type=jnp.float32)


def dot_t(a, b):
    return lax.dot_general(a, b, (((1,), (1,)), ((), ())), preferred_element_type=jnp.float32)


def each(count, body):
    if count <= UNROLL_LIMIT:
        for j in range(count):
            body(j)
    else:
        lax.fori_loop(0, count, lambda j, c: (body(j), c)[1], 0)


def kernel(
    n_vec, n_wlk, vecs, pieces,
    chol_hbm, orb_hbm, logw, par, prop_hbm,
    out_ref, outlog_ref,
    orb, prop, propb, pop, turned, shared, acc,
    load_sem, own_sem, recv, d_send, u_send, r_send, x_send, s_send, p_recv, px_send, ps_send,
    up_ready, x_ready, sib_ready,
):
    me = lax.axis_index("vec")
    mw = lax.axis_index("wlk")
    occ, basis = orb.shape
    rows = vecs * occ
    share = rows // n_wlk
    step = share // pieces
    n_chip = n_wlk // 2
    chip, core = lax.div(mw, 2), lax.rem(mw, 2)
    sibling = mw + 1 - 2 * core
    others = n_vec - 1
    scale = 1.0 / math.sqrt(vecs * n_vec)

    def remote(src_ref, dst_ref, send, recv, where):
        return pltpu.make_async_remote_copy(
            src_ref=src_ref, dst_ref=dst_ref, send_sem=send, recv_sem=recv,
            device_id=where, device_id_type=MESH)

    def at(w, k):
        return pl.ds(pl.multiple_of(w * share + k * step, step), step)

    def quarter(w):
        return pl.ds(pl.multiple_of(w * share, share), share)

    def peer(j):
        return lax.rem(chip + 1 + j, n_chip) * 2 + core

    def down(dst, k):
        return remote(chol_hbm.at[at(mw, k)], shared.at[me, at(mw, k)],
                      d_send.at[dst], recv.at[me, mw, k], {"vec": dst})

    def up_own(k):
        return remote(chol_hbm.at[at(mw, k)], shared.at[me, at(mw, k)],
                      u_send.at[me], recv.at[me, mw, k], {"vec": me + 1})

    def up_relay(src, k):
        return remote(shared.at[src, at(mw, k)], shared.at[src, at(mw, k)],
                      u_send.at[src], recv.at[src, mw, k], {"vec": me + 1})

    def down_relay(k):
        return remote(shared.at[2, at(mw, k)], shared.at[2, at(mw, k)],
                      r_send, recv.at[2, mw, k], {"vec": 0})

    def across(src, w, k):
        return remote(shared.at[src, at(mw, k)], shared.at[src, at(mw, k)],
                      x_send.at[src, w], recv.at[src, mw, k], {"wlk": w})

    def beside(src, w, k):
        return remote(shared.at[src, at(w, k)], shared.at[src, at(w, k)],
                      s_send.at[src, w], recv.at[src, w, k], {"wlk": sibling})

    def arrived(src, w, k):
        remote(shared.at[src, at(w, k)], shared.at[src, at(w, k)],
               s_send.at[src, w], recv.at[src, w, k], {"wlk": sibling}).wait_recv()

    def walker_across(w):
        return remote(pop.at[mw], pop.at[mw], px_send.at[w], p_recv.at[mw], {"wlk": w})

    def walker_beside(w):
        return remote(pop.at[w], pop.at[w], ps_send.at[w], p_recv.at[w], {"wlk": sibling})

    def own_copy():
        return pltpu.make_async_copy(chol_hbm, shared.at[me], own_sem)

    load_orb = pltpu.make_async_copy(orb_hbm, orb, load_sem.at[0])
    load_prop = pltpu.make_async_copy(prop_hbm, prop, load_sem.at[1])

    barrier = pltpu.get_barrier_semaphore()
    for i in range(1, n_vec):
        @pl.when(i > me)
        def _():
            pl.semaphore_signal(barrier, inc=1, device_id={"vec": i}, device_id_type=MESH)
    for i in range(1, n_chip):
        @pl.when(i > chip)
        def _():
            pl.semaphore_signal(barrier, inc=1, device_id={"wlk": i * 2 + core}, device_id_type=MESH)

    @pl.when(core == 0)
    def _():
        pl.semaphore_signal(barrier, inc=1, device_id={"wlk": sibling}, device_id_type=MESH)

    load_orb.start()
    own_copy().start()
    load_prop.start()
    before = me + chip + core

    @pl.when(before > 0)
    def _():
        pl.semaphore_wait(barrier, before)

    relayed = n_vec >= 3

    def goes_down(d):
        return (d < me) & ((d != 0) | (me != 2)) if relayed else d < me

    for d in range(n_vec - 1):
        @pl.when(goes_down(d))
        def _():
            for k in range(pieces):
                down(d, k).start()

    @pl.when(me > 0)
    def _():
        pl.semaphore_signal(up_ready, inc=1, device_id={"vec": me - 1}, device_id_type=MESH)
    for i in range(n_chip - 1):
        @pl.when(i < chip)
        def _():
            pl.semaphore_signal(
                x_ready.at[chip], inc=1, device_id={"wlk": i * 2 + core}, device_id_type=MESH)

    @pl.when(core == 1)
    def _():
        pl.semaphore_signal(sib_ready, inc=1, device_id={"wlk": sibling}, device_id_type=MESH)

    load_orb.wait()
    pop[mw, 0:occ] = orb[...].astype(jnp.bfloat16)
    whole = jnp.full((EXTRA, basis), logw[0], jnp.float32)
    high = whole.astype(jnp.bfloat16)
    rest = whole - high.astype(jnp.float32)
    middle = rest.astype(jnp.bfloat16)
    low = (rest - middle.astype(jnp.float32)).astype(jnp.bfloat16)
    lane = lax.broadcasted_iota(jnp.int32, (EXTRA, basis), 1)
    pop[mw, occ:occ + EXTRA] = jnp.where(
        lane == 0, high.astype(jnp.float32),
        jnp.where(lane == 1, middle.astype(jnp.float32),
                  jnp.where(lane == 2, low.astype(jnp.float32), 0.0))).astype(jnp.bfloat16)
    for i in range(1, n_chip):
        @pl.when(i > chip)
        def _():
            pl.semaphore_wait(x_ready.at[i], 1)
    for j in range(n_chip - 1):
        walker_across(peer(j)).start()

    @pl.when(core == 0)
    def _():
        pl.semaphore_wait(sib_ready, 1)
    walker_beside(mw).start()

    @pl.when(me < n_vec - 1)
    def _():
        pl.semaphore_wait(up_ready, 1)
        for k in range(pieces):
            up_own(k).start()

    load_prop.wait()
    propb[...] = prop[...].T.astype(jnp.bfloat16)

    def source(j):
        lower = me - 1 - j
        return jnp.where(lower >= 0, lower, j + 1) if isinstance(j, int) else lax.select(
            lower >= 0, lower, j + 1)

    def take(j, k):
        src = source(j)
        arrived(src, mw, k)
        for i in range(n_chip - 1):
            across(src, peer(i), k).start()
        beside(src, mw, k).start()

        @pl.when((src < me) & (me < n_vec - 1))
        def _():
            up_relay(src, k).start()
        if relayed:
            @pl.when((src == 2) & (me == 1))
            def _():
                down_relay(k).start()

    def pass_on(j, k):
        src = source(j)
        for i in range(n_chip - 1):
            arrived(src, peer(i), k)
            beside(src, peer(i), k).start()

    for j in range(n_chip - 1):
        remote(pop.at[peer(j)], pop.at[peer(j)], ps_send.at[peer(j)], p_recv.at[peer(j)],
               {"wlk": sibling}).wait_recv()
        walker_beside(peer(j)).start()
    for j in range(n_chip):
        other = lax.rem(chip + j, n_chip) * 2 + 1 - core
        remote(pop.at[other], pop.at[other], ps_send.at[other], p_recv.at[other],
               {"wlk": sibling}).wait_recv()
    parent = par[0]
    rows_of = jnp.full((occ + EXTRA, basis), parent, jnp.int32)
    picked = pop[0].astype(jnp.float32)
    for m in range(1, n_wlk):
        picked = jnp.where(rows_of == m, pop[m].astype(jnp.float32), picked)
    theta = picked[0:occ]
    extra = picked[occ:occ + 8, 0:128]
    chosen_log = jnp.sum(extra, axis=1, keepdims=True)
    turned[...] = theta.T.astype(jnp.bfloat16)
    acc[...] = jnp.zeros_like(acc)

    row = lax.broadcasted_iota(jnp.int32, (occ, occ), 0)
    col = lax.broadcasted_iota(jnp.int32, (occ, occ), 1)
    diagonal = row == col

    def work(src, first, count):
        vectors = shared[src, first * occ:(first + count) * occ] if isinstance(first, int) else shared[
            src, pl.ds(pl.multiple_of(first * occ, occ), count * occ)]
        s = dot(vectors, turned[...])
        blocks = []
        for g in range(count):
            sg = s[g * occ:(g + 1) * occ, :]
            on_diagonal = jnp.where(diagonal, sg, 0.0)
            tg = jnp.sum(jnp.sum(on_diagonal, axis=0, keepdims=True), axis=1, keepdims=True)
            blocks.append((scale * (jnp.where(diagonal, tg, 0.0) - sg)).astype(jnp.bfloat16))
        adjoint = jnp.concatenate(blocks, axis=1) if count > 1 else blocks[0]
        acc[...] += dot(adjoint, vectors)

    own_copy().wait()
    work(me, 0, vecs)

    near = n_chip == 2 and vecs % 2 == 0
    half = vecs // 2

    def near_part(j):
        src = source(j)
        for k in range(pieces):
            arrived(src, sibling, k)
        work(src, chip * half, half)

    def far_part(j):
        src = source(j)
        for k in range(pieces):
            arrived(src, (1 - chip) * 2 + 1 - core, k)
        work(src, (1 - chip) * half, half)

    def all_parts(j):
        src = source(j)
        for i in range(n_chip):
            for k in range(pieces):
                arrived(src, lax.rem(chip + i, n_chip) * 2 + 1 - core, k)
        work(src, 0, vecs)

    if near and others <= UNROLL_LIMIT:
        for j in range(others + 2):
            for k in range(pieces):
                if j < others:
                    take(j, k)
                if 1 <= j <= others:
                    pass_on(j - 1, k)
            if 1 <= j <= others:
                near_part(j - 1)
            if j >= 2:
                far_part(j - 2)
    else:
        def one(j):
            for k in range(pieces):
                take(j, k)
            for k in range(pieces):
                pass_on(j, k)
            all_parts(j)

        each(others, one)

    gradient = acc[...]
    energy = 0.5 * jnp.sum(jnp.sum(theta * gradient, axis=0, keepdims=True), axis=1, keepdims=True)
    outlog_ref[...] = jnp.broadcast_to(chosen_log - energy_step * energy, (8, 128))
    stepped = theta - gradient_step * gradient
    x = dot(stepped.astype(jnp.bfloat16), propb[...])
    mean_square = jnp.sum(jnp.sum(x * x, axis=0, keepdims=True), axis=1, keepdims=True)
    mean_square = mean_square / (occ * basis)
    norm = 1.0 / jnp.sqrt(mean_square + epsilon)
    for it in range(NS_ITERS):
        xb = x.astype(jnp.bfloat16)
        inter = dot_t(xb, xb) * (norm * norm / basis if it == 0 else 1.0 / basis)
        x = 0.5 * (3.0 * x - dot(inter.astype(jnp.bfloat16), xb))
        if it == 0:
            x = norm * x
    out_ref[...] = x

    def sent(send):
        remote(shared.at[0, quarter(0)], shared.at[0, quarter(0)], send, recv.at[0, 0, 0],
               {"wlk": sibling}).wait_send()

    for d in range(n_vec - 1):
        pl.when(goes_down(d))(lambda: sent(d_send.at[d]))

    @pl.when(me < n_vec - 1)
    def _():
        sent(u_send.at[me])

    def drain(j):
        src = source(j)
        pl.when((src < me) & (me < n_vec - 1))(lambda: sent(u_send.at[src]))
        for i in range(n_chip - 1):
            sent(x_send.at[src, peer(i)])
        for i in range(n_chip):
            sent(s_send.at[src, lax.rem(chip + i, n_chip) * 2 + core])

    each(others, drain)
    if relayed:
        pl.when(me == 1)(lambda: sent(r_send))
    for j in range(n_chip - 1):
        walker_across(peer(j)).wait_send()
    for j in range(n_chip):
        walker_beside(lax.rem(chip + j, n_chip) * 2 + core).wait_send()


def deliver(x_ref, log_ref, out_ref, outlog_ref, sem):
    copies = [
        pltpu.make_async_copy(log_ref.at[0:1], outlog_ref, sem.at[0]),
        pltpu.make_async_copy(x_ref, out_ref, sem.at[1]),
    ]
    for copy in copies:
        copy.start()
    for copy in copies:
        copy.wait()


def solution(mesh):
    n_vec, n_wlk = mesh.shape["vec"], mesh.shape["wlk"]

    def local(cholesky, orbitals, log_weights, parents, propagator):
        walkers, occ, basis = orbitals.shape
        assert walkers == 1 and n_wlk % 2 == 0
        vecs = cholesky.shape[0]
        share = vecs * occ // n_wlk
        assert share * n_wlk == vecs * occ
        pieces = PIECES if n_vec <= UNROLL_LIMIT and share % (16 * PIECES) == 0 else 1
        f32, bf16 = jnp.float32, jnp.bfloat16
        dma = pltpu.SemaphoreType.DMA
        regular = pltpu.SemaphoreType.REGULAR
        hbm = pl.BlockSpec(memory_space=pltpu.HBM)
        smem = pl.BlockSpec(memory_space=pltpu.SMEM)
        vmem = pl.BlockSpec(memory_space=pltpu.VMEM)
        x, logs = pl.pallas_call(
            functools.partial(kernel, n_vec, n_wlk, vecs, pieces),
            out_shape=(pltpu.VMEM((occ, basis), f32), pltpu.VMEM((8, 128), f32)),
            in_specs=[hbm, hbm, smem, smem, hbm],
            out_specs=(vmem, vmem),
            scratch_shapes=[
                pltpu.VMEM((occ, basis), f32),
                pltpu.VMEM(propagator.shape, f32),
                pltpu.VMEM(propagator.shape, bf16),
                pltpu.VMEM((n_wlk, occ + EXTRA, basis), bf16),
                pltpu.VMEM((basis, occ), bf16),
                pltpu.VMEM((n_vec, vecs * occ, basis), bf16),
                pltpu.VMEM((occ, basis), f32),
                dma((2,)), dma, dma((n_vec, n_wlk, pieces)),
                dma((n_vec,)), dma((n_vec,)), dma, dma((n_vec, n_wlk)), dma((n_vec, n_wlk)),
                dma((n_wlk,)), dma((n_wlk,)), dma((n_wlk,)),
                regular, regular((n_wlk // 2,)), regular,
            ],
            compiler_params=pltpu.CompilerParams(
                collective_id=0, has_side_effects=True, vmem_limit_bytes=60000000),
        )(
            cholesky.reshape(vecs * occ, basis),
            orbitals.reshape(occ, basis),
            log_weights,
            parents,
            propagator,
        )

        def here(array):
            return pltpu.with_memory_space_constraint(array, pltpu.VMEM)

        out, log = pl.pallas_call(
            deliver,
            out_shape=(
                jax.ShapeDtypeStruct((occ, basis), f32),
                jax.ShapeDtypeStruct((1, 128), f32),
            ),
            in_specs=[vmem, vmem],
            out_specs=(hbm, hbm),
            scratch_shapes=[dma((2,))],
        )(here(x), here(logs))
        return out.reshape(orbitals.shape), log[0, :1]

    placed = (
        P(("grp", "vec"), None, None),
        P(("grp", "vec", "wlk"), None, None),
        P(("grp", "vec", "wlk")),
        P(("grp", "vec", "wlk")),
        P("grp", None),
    )
    return jax.shard_map(
        local,
        mesh=mesh,
        in_specs=placed,
        out_specs=(P(("grp", "vec", "wlk"), None, None), P(("grp", "vec", "wlk"))),
        check_vma=False,
    )
```

time: 26.3 us -> 26.1 us (level)
  the two profiles are of different devices: /device:TPU:1 before, /device:TPU:0 now
where the time goes in v1:
time: 26.1 us; the launch traced here: 26 us
  Pallas kernels  24 us (92%)
  between operations  1.93 us (7%)
    pallas_call x1, Pallas kernels, local(): pl.pallas_call(functools.partial(kernel, n_vec, n_wlk, vecs, pieces), out...  23.4 us
    pallas_call x1, Pallas kernels, local(): pl.pallas_call(deliver, out_shape=(jax.ShapeDtypeStruct((occ, basis), f32...  0.68 us

profile of v1, /device:TPU:0, one launch (start us, length us, event | category | flops | bytes accessed | tf_op | source)
XLA Modules:
  0.0 26.0 jit_solution(7808912652754305422)
XLA Ops:
  1.9 23.4 %shard_map.68 = (f32[64,512]{1,0:T(8,128)S(1)}, f32[8,128]{1,0:T(8,128)S(1)}) custom-call(bf16[384,512]{1,0:T(8,128)(2,1)} %bitcast.5, f32[64,512]{1,0:T(8,128)} %bitcast.6, f32[1]{0:T(128)S(6)} %copy.7.logw, s32[1]{0:T(128)S(6)} %copy.8.par, f32[512,512]{1,0:T(8,128)} %prop_hbm.1), custom_call_target="tpu_custom_call" | custom-call | tf_op jit(solution)/shard_map/pallas_call | solution.py:372
  25.3 0.7 %shard_map.69 = (f32[64,512]{1,0:T(8,128)}, f32[1,128]{1,0:T(1,128)}) custom-call(f32[64,512]{1,0:T(8,128)S(1)} %get-tuple-element.6.x_ref, f32[8,128]{1,0:T(8,128)S(1)} %get-tuple-element.7.log_ref), custom_call_target="tpu_custom_call" | custom-call | tf_op jit(solution)/shard_map/pallas_call | solution.py:403

commit v2 on v1

v2 whole, which is shorter than its diff:
```python
import functools
import math

import jax
import jax.numpy as jnp
from jax import lax
from jax.experimental import pallas as pl
from jax.experimental.pallas import tpu as pltpu
from jax.sharding import PartitionSpec as P

NS_ITERS = 2

gradient_step = 0.25
energy_step = 0.002
epsilon = 1e-06

MESH = pl.DeviceIdType.MESH
UNROLL_LIMIT = 8
PIECES = 3
EXTRA = 16


def dot(a, b):
    return lax.dot_general(a, b, (((1,), (0,)), ((), ())), preferred_element_type=jnp.float32)


def dot_t(a, b):
    return lax.dot_general(a, b, (((1,), (1,)), ((), ())), preferred_element_type=jnp.float32)


def each(count, body):
    if count <= UNROLL_LIMIT:
        for j in range(count):
            body(j)
    else:
        lax.fori_loop(0, count, lambda j, c: (body(j), c)[1], 0)


def kernel(
    n_vec, n_wlk, vecs, pieces,
    chol_hbm, orb_hbm, logw, par, prop_hbm,
    out_ref, outlog_ref,
    orb, prop, propb, pop, turned, shared, acc,
    load_sem, z_recv, x_recv, near_recv, far_recv, p_recv, v_send, p_send,
    z_ready, x_ready, sib_ready,
):
    me = lax.axis_index("vec")
    mw = lax.axis_index("wlk")
    occ, basis = orb.shape
    rows = vecs * occ
    share = rows // n_wlk
    step = share // pieces
    n_chip = n_wlk // 2
    chip, core = lax.div(mw, 2), lax.rem(mw, 2)
    sibling = mw + 1 - 2 * core
    others, chips = n_vec - 1, n_chip - 1
    scale = 1.0 / math.sqrt(vecs * n_vec)

    def remote(src_ref, dst_ref, send, recv, where):
        return pltpu.make_async_remote_copy(
            src_ref=src_ref, dst_ref=dst_ref, send_sem=send, recv_sem=recv,
            device_id=where, device_id_type=MESH)

    def at(w, k):
        return pl.ds(pl.multiple_of(w * share + k * step, step), step)

    def quarter(w):
        return pl.ds(pl.multiple_of(w * share, share), share)

    def slot(src, dst):
        return jnp.where(src > dst, src - 1, src)

    def peer(i):
        return lax.rem(chip + 1 + i, n_chip) * 2 + core

    def source(j):
        lower = me - 1 - j
        return jnp.where(lower >= 0, lower, j + 1)

    def along(dst, k):
        return remote(chol_hbm.at[at(mw, k)], shared.at[me, at(mw, k)],
                      v_send, z_recv.at[slot(me, dst), k], {"vec": dst})

    def from_along(src, k):
        remote(shared.at[src, at(mw, k)], shared.at[src, at(mw, k)],
               v_send, z_recv.at[slot(src, me), k], {"wlk": sibling}).wait_recv()

    def across(src, i, k):
        return remote(shared.at[src, at(mw, k)], shared.at[src, at(mw, k)],
                      v_send, x_recv.at[slot(src, me), chips - 1 - i, k], {"wlk": peer(i)})

    def from_across(src, i, k):
        remote(shared.at[src, at(peer(i), k)], shared.at[src, at(peer(i), k)],
               v_send, x_recv.at[slot(src, me), i, k], {"wlk": sibling}).wait_recv()

    def beside(src, k):
        return remote(shared.at[src, at(mw, k)], shared.at[src, at(mw, k)],
                      v_send, near_recv.at[slot(src, me)], {"wlk": sibling})

    def from_beside(src):
        remote(shared.at[src, quarter(sibling)], shared.at[src, quarter(sibling)],
               v_send, near_recv.at[slot(src, me)], {"wlk": sibling}).wait_recv()

    def beyond(src, i, k):
        return remote(shared.at[src, at(peer(i), k)], shared.at[src, at(peer(i), k)],
                      v_send, far_recv.at[slot(src, me), i], {"wlk": sibling})

    def from_beyond(src, i):
        w = peer(i) + 1 - 2 * core
        remote(shared.at[src, quarter(w)], shared.at[src, quarter(w)],
               v_send, far_recv.at[slot(src, me), i], {"wlk": sibling}).wait_recv()

    def walker(w, index, where):
        return remote(pop.at[w], pop.at[w], p_send, p_recv.at[index], {"wlk": where})

    load_orb = pltpu.make_async_copy(orb_hbm, orb, load_sem.at[0])
    load_own = pltpu.make_async_copy(chol_hbm, shared.at[me], load_sem.at[1])
    load_prop = pltpu.make_async_copy(prop_hbm, prop, load_sem.at[2])

    barrier = pltpu.get_barrier_semaphore()

    def greet(semaphore, where):
        pl.semaphore_signal(semaphore, inc=1, device_id=where, device_id_type=MESH)

    each(others, lambda j: pl.when(j + 1 > me)(lambda: greet(barrier, {"vec": j + 1})))
    each(chips, lambda j: pl.when(j + 1 > chip)(
        lambda: greet(barrier, {"wlk": (j + 1) * 2 + core})))
    pl.when(core == 0)(lambda: greet(barrier, {"wlk": sibling}))

    load_orb.start()
    before = me + chip + core
    pl.when(before > 0)(lambda: pl.semaphore_wait(barrier, before))

    each(others, lambda j: pl.when(j < me)(lambda: greet(z_ready.at[me - 1], {"vec": j})))
    each(chips, lambda j: pl.when(j < chip)(
        lambda: greet(x_ready.at[chip - 1], {"wlk": j * 2 + core})))
    pl.when(core == 1)(lambda: greet(sib_ready, {"wlk": sibling}))

    def send_along(dst):
        for k in range(pieces):
            along(dst, k).start()

    each(others, lambda j: pl.when(j < me)(lambda: send_along(j)))
    load_own.start()
    load_prop.start()

    load_orb.wait()
    pop[mw, 0:occ] = orb[...].astype(jnp.bfloat16)
    whole = jnp.full((EXTRA, basis), logw[0], jnp.float32)
    high = whole.astype(jnp.bfloat16).astype(jnp.float32)
    middle = (whole - high).astype(jnp.bfloat16).astype(jnp.float32)
    low = whole - high - middle
    lane = lax.broadcasted_iota(jnp.int32, (EXTRA, basis), 1)
    pop[mw, occ:occ + EXTRA] = jnp.where(
        lane == 0, high,
        jnp.where(lane == 1, middle, jnp.where(lane == 2, low, 0.0))).astype(jnp.bfloat16)

    pl.when(core == 0)(lambda: pl.semaphore_wait(sib_ready, 1))
    walker(mw, 2 * chips, sibling).start()
    each(chips, lambda j: pl.when(j + 1 > chip)(lambda: pl.semaphore_wait(x_ready.at[j], 1)))
    for i in range(chips):
        walker(mw, chips - 1 - i, peer(i)).start()

    def send_up(j):
        @pl.when(me + j + 1 < n_vec)
        def _():
            pl.semaphore_wait(z_ready.at[me + j], 1)
            send_along(me + j + 1)

    def take(j, k):
        src = source(j)
        from_along(src, k)
        for i in range(chips):
            across(src, i, k).start()
        beside(src, k).start()

    def pass_on(j, k):
        src = source(j)
        for i in range(chips):
            from_across(src, i, k)
            beyond(src, i, k).start()

    def pass_walkers():
        for i in range(chips):
            walker(peer(i), i, sibling).wait_recv()
            walker(peer(i), chips + i, sibling).start()

    def all_walkers():
        for i in range(chips + 1):
            w = peer(i) + 1 - 2 * core
            walker(w, chips + i, sibling).wait_recv()

    row = lax.broadcasted_iota(jnp.int32, (occ, occ), 0)
    col = lax.broadcasted_iota(jnp.int32, (occ, occ), 1)
    diagonal = row == col

    def work(src, first, count):
        vectors = shared[src, pl.ds(pl.multiple_of(first * occ, occ), count * occ)]
        s = dot(vectors, turned[...])
        blocks = []
        for g in range(count):
            sg = s[g * occ:(g + 1) * occ, :]
            on_diagonal = jnp.where(diagonal, sg, 0.0)
            tg = jnp.sum(jnp.sum(on_diagonal, axis=0, keepdims=True), axis=1, keepdims=True)
            blocks.append((scale * (jnp.where(diagonal, tg, 0.0) - sg)).astype(jnp.bfloat16))
        adjoint = jnp.concatenate(blocks, axis=1) if count > 1 else blocks[0]
        acc[...] += dot(adjoint, vectors)

    def choose():
        rows_of = jnp.full((occ + EXTRA, basis), par[0], jnp.int32)
        picked = pop[0].astype(jnp.float32)
        for m in range(1, n_wlk):
            picked = jnp.where(rows_of == m, pop[m].astype(jnp.float32), picked)
        turned[...] = picked[0:occ].T.astype(jnp.bfloat16)
        orb[...] = picked[0:occ]
        outlog_ref[...] = jnp.broadcast_to(
            jnp.sum(picked[occ:occ + 8, 0:128], axis=1, keepdims=True), (8, 128))
        acc[...] = jnp.zeros_like(acc)

    def turn_propagator():
        load_prop.wait()
        propb[...] = prop[...].T.astype(jnp.bfloat16)

    half = vecs // 2

    def near_part(j):
        from_beside(source(j))
        work(source(j), chip * half, half)

    def far_part(j):
        from_beyond(source(j), 0)
        work(source(j), (1 - chip) * half, half)

    if n_chip == 2 and vecs % 2 == 0 and 2 <= others <= UNROLL_LIMIT:
        send_up(0)
        for k in range(pieces):
            take(0, k)
        send_up(1)
        pass_walkers()
        turn_propagator()
        all_walkers()
        choose()
        load_own.wait()
        work(me, 0, half)
        for j in range(2, others):
            send_up(j)
        for j in range(1, others + 2):
            for k in range(pieces):
                if j < others:
                    take(j, k)
                if j <= others:
                    pass_on(j - 1, k)
                if k == 0:
                    if j == 1:
                        work(me, half, half)
                    else:
                        far_part(j - 2)
            if j <= others:
                near_part(j - 1)
    else:
        each(others, send_up)
        pass_walkers()
        turn_propagator()
        all_walkers()
        choose()
        load_own.wait()
        work(me, 0, vecs)

        def one(j):
            for k in range(pieces):
                take(j, k)
            for k in range(pieces):
                pass_on(j, k)
            from_beside(source(j))
            for i in range(chips):
                from_beyond(source(j), i)
            work(source(j), 0, vecs)

        each(others, one)

    theta = orb[...]
    gradient = acc[...]
    energy = 0.5 * jnp.sum(jnp.sum(theta * gradient, axis=0, keepdims=True), axis=1, keepdims=True)
    outlog_ref[...] -= energy_step * jnp.broadcast_to(energy, (8, 128))
    stepped = theta - gradient_step * gradient
    x = dot(stepped.astype(jnp.bfloat16), propb[...])
    mean_square = jnp.sum(jnp.sum(x * x, axis=0, keepdims=True), axis=1, keepdims=True)
    mean_square = mean_square / (occ * basis)
    norm = 1.0 / jnp.sqrt(mean_square + epsilon)
    for it in range(NS_ITERS):
        xb = x.astype(jnp.bfloat16)
        inter = dot_t(xb, xb) * (norm * norm / basis if it == 0 else 1.0 / basis)
        x = 0.5 * (3.0 * x - dot(inter.astype(jnp.bfloat16), xb))
        if it == 0:
            x = norm * x
    out_ref[...] = x

    every = shared.at[pl.ds(0, others)]
    remote(every, every, v_send, v_send, {"wlk": sibling}).wait_send()
    walkers = pop.at[pl.ds(0, n_wlk - 1)]
    remote(walkers, walkers, p_send, p_send, {"wlk": sibling}).wait_send()


def deliver(x_ref, log_ref, out_ref, outlog_ref, sem):
    copies = [
        pltpu.make_async_copy(log_ref.at[0:1], outlog_ref, sem.at[0]),
        pltpu.make_async_copy(x_ref, out_ref, sem.at[1]),
    ]
    for copy in copies:
        copy.start()
    for copy in copies:
        copy.wait()


def solution(mesh):
    n_vec, n_wlk = mesh.shape["vec"], mesh.shape["wlk"]

    def local(cholesky, orbitals, log_weights, parents, propagator):
        walkers, occ, basis = orbitals.shape
        assert walkers == 1 and n_wlk % 2 == 0
        vecs = cholesky.shape[0]
        share = vecs * occ // n_wlk
        assert share * n_wlk == vecs * occ
        pieces = PIECES if n_vec <= UNROLL_LIMIT and share % (16 * PIECES) == 0 else 1
        others, chips = n_vec - 1, n_wlk // 2 - 1
        f32, bf16 = jnp.float32, jnp.bfloat16
        dma = pltpu.SemaphoreType.DMA
        regular = pltpu.SemaphoreType.REGULAR
        hbm = pl.BlockSpec(memory_space=pltpu.HBM)
        smem = pl.BlockSpec(memory_space=pltpu.SMEM)
        vmem = pl.BlockSpec(memory_space=pltpu.VMEM)
        x, logs = pl.pallas_call(
            functools.partial(kernel, n_vec, n_wlk, vecs, pieces),
            out_shape=(pltpu.VMEM((occ, basis), f32), pltpu.VMEM((8, 128), f32)),
            in_specs=[hbm, hbm, smem, smem, hbm],
            out_specs=(vmem, vmem),
            scratch_shapes=[
                pltpu.VMEM((occ, basis), f32),
                pltpu.VMEM(propagator.shape, f32),
                pltpu.VMEM(propagator.shape, bf16),
                pltpu.VMEM((n_wlk, occ + EXTRA, basis), bf16),
                pltpu.VMEM((basis, occ), bf16),
                pltpu.VMEM((n_vec, vecs * occ, basis), bf16),
                pltpu.VMEM((occ, basis), f32),
                dma((3,)),
                dma((others, pieces)), dma((others, chips, pieces)), dma((others,)), dma((others, chips)),
                dma((2 * chips + 1,)), dma, dma,
                regular((others,)), regular((chips,)), regular,
            ],
            compiler_params=pltpu.CompilerParams(
                collective_id=0, has_side_effects=True, vmem_limit_bytes=60000000),
        )(
            cholesky.reshape(vecs * occ, basis),
            orbitals.reshape(occ, basis),
            log_weights,
            parents,
            propagator,
        )

        def here(array):
            return pltpu.with_memory_space_constraint(array, pltpu.VMEM)

        out, log = pl.pallas_call(
            deliver,
            out_shape=(
                jax.ShapeDtypeStruct((occ, basis), f32),
                jax.ShapeDtypeStruct((1, 128), f32),
            ),
            in_specs=[vmem, vmem],
            out_specs=(hbm, hbm),
            scratch_shapes=[dma((2,))],
        )(here(x), here(logs))
        return out.reshape(orbitals.shape), log[0, :1]

    placed = (
        P(("grp", "vec"), None, None),
        P(("grp", "vec", "wlk"), None, None),
        P(("grp", "vec", "wlk")),
        P(("grp", "vec", "wlk")),
        P("grp", None),
    )
    return jax.shard_map(
        local,
        mesh=mesh,
        in_specs=placed,
        out_specs=(P(("grp", "vec", "wlk"), None, None), P(("grp", "vec", "wlk"))),
        check_vma=False,
    )
```

time: 26.1 us -> 23.8 us (0.912)
  the two profiles are of different devices: /device:TPU:0 before, /device:TPU:1 now
where the time goes in v2:
time: 23.8 us; the launch traced here: 23.7 us
  Pallas kernels  21.7 us (91%)
  between operations  1.93 us (8%)
    pallas_call x1, Pallas kernels, local(): pl.pallas_call(functools.partial(kernel, n_vec, n_wlk, vecs, pieces), out...  21.1 us
    pallas_call x1, Pallas kernels, local(): pl.pallas_call(deliver, out_shape=(jax.ShapeDtypeStruct((occ, basis), f32...  0.68 us

profile of v2, /device:TPU:1, one launch (start us, length us, event | category | flops | bytes accessed | tf_op | source)
XLA Modules:
  0.0 23.7 jit_solution(3041807466354519217)
XLA Ops:
  1.9 21.1 %shard_map.68 = (f32[64,512]{1,0:T(8,128)S(1)}, f32[8,128]{1,0:T(8,128)S(1)}) custom-call(bf16[384,512]{1,0:T(8,128)(2,1)} %bitcast.5, f32[64,512]{1,0:T(8,128)} %bitcast.6, f32[1]{0:T(128)S(6)} %copy.7.logw, s32[1]{0:T(128)S(6)} %copy.8.par, f32[512,512]{1,0:T(8,128)} %prop_hbm.1), custom_call_target="tpu_custom_call" | custom-call | tf_op jit(solution)/shard_map/pallas_call | solution.py:332
  23.0 0.7 %shard_map.69 = (f32[64,512]{1,0:T(8,128)}, f32[1,128]{1,0:T(1,128)}) custom-call(f32[64,512]{1,0:T(8,128)S(1)} %get-tuple-element.6.x_ref, f32[8,128]{1,0:T(8,128)S(1)} %get-tuple-element.7.log_ref), custom_call_target="tpu_custom_call" | custom-call | tf_op jit(solution)/shard_map/pallas_call | solution.py:363

commit v3 on v2

--- a/solution.py
+++ b/solution.py
@@ -16,8 +16,8 @@
 
 MESH = pl.DeviceIdType.MESH
 UNROLL_LIMIT = 8
-PIECES = 3
 EXTRA = 16
+ORDER = ((2, 3, 1), (0, 3, 2), (3, 0, 1), (2, 0, 1))
 
 
 def dot(a, b):
@@ -37,11 +37,11 @@
 
 
 def kernel(
-    n_vec, n_wlk, vecs, pieces,
+    n_vec, n_wlk, vecs, pieces, paired,
     chol_hbm, orb_hbm, logw, par, prop_hbm,
     out_ref, outlog_ref,
-    orb, prop, propb, pop, turned, shared, acc,
-    load_sem, z_recv, x_recv, near_recv, far_recv, p_recv, v_send, p_send,
+    orb, prop, propb, pop, turned, shared, acc, gsend, grecv,
+    load_sem, z_recv, x_recv, near_recv, far_recv, p_recv, g_recv, v_send, p_send, g_send,
     z_ready, x_ready, sib_ready,
 ):
     me = lax.axis_index("vec")
@@ -74,6 +74,12 @@
         return lax.rem(chip + 1 + i, n_chip) * 2 + core
 
     def source(j):
+        if n_vec == 4:
+            first, *rest = (order[j] for order in ORDER)
+            src = first
+            for i, other in enumerate(rest):
+                src = jnp.where(me == i + 1, other, src)
+            return src
         lower = me - 1 - j
         return jnp.where(lower >= 0, lower, j + 1)
 
@@ -140,9 +146,19 @@
         for k in range(pieces):
             along(dst, k).start()
 
-    each(others, lambda j: pl.when(j < me)(lambda: send_along(j)))
+    if n_vec == 4:
+        pl.when(me == 3)(lambda: send_along(2))
+    each(others, lambda j: pl.when((j < me) & ((n_vec != 4) | (j != 2)))(lambda: send_along(j)))
     load_own.start()
     load_prop.start()
+
+    def send_up(j):
+        @pl.when(me + j + 1 < n_vec)
+        def _():
+            pl.semaphore_wait(z_ready.at[me + j], 1)
+            send_along(me + j + 1)
+
+    send_up(0)
 
     load_orb.wait()
     pop[mw, 0:occ] = orb[...].astype(jnp.bfloat16)
@@ -151,21 +167,16 @@
     middle = (whole - high).astype(jnp.bfloat16).astype(jnp.float32)
     low = whole - high - middle
     lane = lax.broadcasted_iota(jnp.int32, (EXTRA, basis), 1)
+    parent = jnp.full((EXTRA, basis), par[0], jnp.int32).astype(jnp.float32)
     pop[mw, occ:occ + EXTRA] = jnp.where(
-        lane == 0, high,
-        jnp.where(lane == 1, middle, jnp.where(lane == 2, low, 0.0))).astype(jnp.bfloat16)
+        lane == 0, high, jnp.where(lane == 1, middle, jnp.where(
+            lane == 2, low, jnp.where(lane == 3, parent, 0.0)))).astype(jnp.bfloat16)
 
     pl.when(core == 0)(lambda: pl.semaphore_wait(sib_ready, 1))
     walker(mw, 2 * chips, sibling).start()
     each(chips, lambda j: pl.when(j + 1 > chip)(lambda: pl.semaphore_wait(x_ready.at[j], 1)))
     for i in range(chips):
         walker(mw, chips - 1 - i, peer(i)).start()
-
-    def send_up(j):
-        @pl.when(me + j + 1 < n_vec)
-        def _():
-            pl.semaphore_wait(z_ready.at[me + j], 1)
-            send_along(me + j + 1)
 
     def take(j, k):
         src = source(j)
@@ -206,15 +217,23 @@
         adjoint = jnp.concatenate(blocks, axis=1) if count > 1 else blocks[0]
         acc[...] += dot(adjoint, vectors)
 
-    def choose():
-        rows_of = jnp.full((occ + EXTRA, basis), par[0], jnp.int32)
+    def pick(w):
+        parent = jnp.broadcast_to(pop[w, occ:occ + 1, 3:4].astype(jnp.float32), (occ + EXTRA, basis))
         picked = pop[0].astype(jnp.float32)
         for m in range(1, n_wlk):
-            picked = jnp.where(rows_of == m, pop[m].astype(jnp.float32), picked)
-        turned[...] = picked[0:occ].T.astype(jnp.bfloat16)
+            picked = jnp.where(parent == m, pop[m].astype(jnp.float32), picked)
+        return picked
+
+    def choose():
+        picked = pick(mw)
         orb[...] = picked[0:occ]
-        outlog_ref[...] = jnp.broadcast_to(
-            jnp.sum(picked[occ:occ + 8, 0:128], axis=1, keepdims=True), (8, 128))
+        logs = picked[occ:occ + 8, 0:128]
+        logs = jnp.where(lax.broadcasted_iota(jnp.int32, (8, 128), 1) < 3, logs, 0.0)
+        outlog_ref[...] = jnp.broadcast_to(jnp.sum(logs, axis=1, keepdims=True), (8, 128))
+        chosen = picked[0:occ]
+        if paired:
+            chosen = jnp.concatenate([chosen, pick(peer(0))[0:occ]], axis=0)
+        turned[...] = chosen.T.astype(jnp.bfloat16)
         acc[...] = jnp.zeros_like(acc)
 
     def turn_propagator():
@@ -222,43 +241,55 @@
         propb[...] = prop[...].T.astype(jnp.bfloat16)
 
     half = vecs // 2
-
-    def near_part(j):
-        from_beside(source(j))
-        work(source(j), chip * half, half)
-
-    def far_part(j):
-        from_beyond(source(j), 0)
-        work(source(j), (1 - chip) * half, half)
-
-    if n_chip == 2 and vecs % 2 == 0 and 2 <= others <= UNROLL_LIMIT:
-        send_up(0)
-        for k in range(pieces):
-            take(0, k)
-        send_up(1)
+    where = lax.broadcasted_iota(jnp.int32, (occ, 2 * occ), 1)
+    left = where < occ
+    pair_diagonal = lax.broadcasted_iota(jnp.int32, (occ, 2 * occ), 0) == jnp.where(
+        left, where, where - occ)
+
+    def work_pair(src, last):
+        vectors = shared[src, pl.ds(pl.multiple_of(chip * half * occ, occ), half * occ)]
+        s = dot(vectors, turned[...])
+        blocks = []
+        for g in range(half):
+            sg = s[g * occ:(g + 1) * occ, :]
+            along_diagonal = jnp.sum(jnp.where(pair_diagonal, sg, 0.0), axis=0, keepdims=True)
+            mine = jnp.sum(jnp.where(left[0:1], along_diagonal, 0.0), axis=1, keepdims=True)
+            theirs = jnp.sum(jnp.where(left[0:1], 0.0, along_diagonal), axis=1, keepdims=True)
+            trace = jnp.where(left, mine, theirs)
+            blocks.append((scale * (jnp.where(pair_diagonal, trace, 0.0) - sg)).astype(jnp.bfloat16))
+        mine = jnp.concatenate([b[:, 0:occ] for b in blocks], axis=1)
+        theirs = jnp.concatenate([b[:, occ:] for b in blocks], axis=1)
+        if last:
+            gsend[...] = (acc[occ:] + dot(theirs, vectors)).astype(jnp.bfloat16)
+            give().start()
+            acc[0:occ] += dot(mine, vectors)
+        else:
+            acc[...] += dot(jnp.concatenate([mine, theirs], axis=0), vectors)
+
+    def give():
+        return remote(gsend, grecv, g_send, g_recv, {"wlk": peer(0)})
+
+    if paired:
+        for j in range(1, others):
+            send_up(j)
         pass_walkers()
         turn_propagator()
         all_walkers()
         choose()
         load_own.wait()
-        work(me, 0, half)
-        for j in range(2, others):
-            send_up(j)
-        for j in range(1, others + 2):
-            for k in range(pieces):
-                if j < others:
-                    take(j, k)
-                if j <= others:
-                    pass_on(j - 1, k)
-                if k == 0:
-                    if j == 1:
-                        work(me, half, half)
-                    else:
-                        far_part(j - 2)
-            if j <= others:
-                near_part(j - 1)
+        work_pair(me, False)
+        for j in range(others):
+            from_along(source(j), 0)
+            beside(source(j), 0).start()
+            if j > 0:
+                from_beside(source(j - 1))
+                work_pair(source(j - 1), False)
+        from_beside(source(others - 1))
+        work_pair(source(others - 1), True)
+        give().wait_recv()
+        acc[0:occ] += grecv[...].astype(jnp.float32)
     else:
-        each(others, send_up)
+        each(others - 1, lambda j: send_up(j + 1))
         pass_walkers()
         turn_propagator()
         all_walkers()
@@ -279,7 +310,7 @@
         each(others, one)
 
     theta = orb[...]
-    gradient = acc[...]
+    gradient = acc[0:occ]
     energy = 0.5 * jnp.sum(jnp.sum(theta * gradient, axis=0, keepdims=True), axis=1, keepdims=True)
     outlog_ref[...] -= energy_step * jnp.broadcast_to(energy, (8, 128))
     stepped = theta - gradient_step * gradient
@@ -295,10 +326,15 @@
             x = norm * x
     out_ref[...] = x
 
-    every = shared.at[pl.ds(0, others)]
-    remote(every, every, v_send, v_send, {"wlk": sibling}).wait_send()
-    walkers = pop.at[pl.ds(0, n_wlk - 1)]
-    remote(walkers, walkers, p_send, p_send, {"wlk": sibling}).wait_send()
+    def sent(view, semaphore):
+        remote(view, view, semaphore, semaphore, {"wlk": sibling}).wait_send()
+
+    if paired:
+        sent(shared.at[pl.ds(0, others), pl.ds(0, 2 * share)], v_send)
+        give().wait_send()
+    else:
+        sent(shared.at[pl.ds(0, others)], v_send)
+    sent(pop.at[pl.ds(0, n_wlk - 1)], p_send)
 
 
 def deliver(x_ref, log_ref, out_ref, outlog_ref, sem):
@@ -316,13 +352,15 @@
     n_vec, n_wlk = mesh.shape["vec"], mesh.shape["wlk"]
 
     def local(cholesky, orbitals, log_weights, parents, propagator):
-        walkers, occ, basis = orbitals.shape
-        assert walkers == 1 and n_wlk % 2 == 0
+        own, occ, basis = orbitals.shape
+        assert own == 1 and n_wlk % 2 == 0
         vecs = cholesky.shape[0]
         share = vecs * occ // n_wlk
         assert share * n_wlk == vecs * occ
-        pieces = PIECES if n_vec <= UNROLL_LIMIT and share % (16 * PIECES) == 0 else 1
+        paired = n_wlk == 4 and vecs % 2 == 0 and 2 <= n_vec <= UNROLL_LIMIT
+        pieces, walkers = 1, 2 if paired else 1
         others, chips = n_vec - 1, n_wlk // 2 - 1
+        crossing = (1, 1) if paired else (others, chips)
         f32, bf16 = jnp.float32, jnp.bfloat16
         dma = pltpu.SemaphoreType.DMA
         regular = pltpu.SemaphoreType.REGULAR
@@ -330,7 +368,7 @@
         smem = pl.BlockSpec(memory_space=pltpu.SMEM)
         vmem = pl.BlockSpec(memory_space=pltpu.VMEM)
         x, logs = pl.pallas_call(
-            functools.partial(kernel, n_vec, n_wlk, vecs, pieces),
+            functools.partial(kernel, n_vec, n_wlk, vecs, pieces, paired),
             out_shape=(pltpu.VMEM((occ, basis), f32), pltpu.VMEM((8, 128), f32)),
             in_specs=[hbm, hbm, smem, smem, hbm],
             out_specs=(vmem, vmem),
@@ -339,12 +377,14 @@
                 pltpu.VMEM(propagator.shape, f32),
                 pltpu.VMEM(propagator.shape, bf16),
                 pltpu.VMEM((n_wlk, occ + EXTRA, basis), bf16),
-                pltpu.VMEM((basis, occ), bf16),
+                pltpu.VMEM((basis, walkers * occ), bf16),
                 pltpu.VMEM((n_vec, vecs * occ, basis), bf16),
-                pltpu.VMEM((occ, basis), f32),
+                pltpu.VMEM((walkers * occ, basis), f32),
+                pltpu.VMEM((occ, basis), bf16),
+                pltpu.VMEM((occ, basis), bf16),
                 dma((3,)),
-                dma((others, pieces)), dma((others, chips, pieces)), dma((others,)), dma((others, chips)),
-                dma((2 * chips + 1,)), dma, dma,
+                dma((others, pieces)), dma(crossing + (pieces,)), dma((others,)), dma(crossing),
+                dma((2 * chips + 1,)), dma, dma, dma, dma,
                 regular((others,)), regular((chips,)), regular,
             ],
             compiler_params=pltpu.CompilerParams(

time: 23.8 us -> 21 us (0.88)
  the two profiles are of different devices: /device:TPU:1 before, /device:TPU:25 now
where the time goes in v3:
time: 21 us; the launch traced here: 20.7 us
  Pallas kernels  18.7 us (89%)
  between operations  1.93 us (9%)
    pallas_call x1, Pallas kernels, local(): pl.pallas_call(functools.partial(kernel, n_vec, n_wlk, vecs, pieces, pair...  18.1 us
    pallas_call x1, Pallas kernels, local(): pl.pallas_call(deliver, out_shape=(jax.ShapeDtypeStruct((occ, basis), f32...  0.68 us

profile of v3, /device:TPU:25, one launch (start us, length us, event | category | flops | bytes accessed | tf_op | source)
XLA Modules:
  0.0 20.7 jit_solution(9379559851394341051)
XLA Ops:
  1.9 18.1 %shard_map.68 = (f32[64,512]{1,0:T(8,128)S(1)}, f32[8,128]{1,0:T(8,128)S(1)}) custom-call(bf16[384,512]{1,0:T(8,128)(2,1)} %bitcast.5, f32[64,512]{1,0:T(8,128)} %bitcast.6, f32[1]{0:T(128)S(6)} %copy.7.logw, s32[1]{0:T(128)S(6)} %copy.8.par, f32[512,512]{1,0:T(8,128)} %prop_hbm.1), custom_call_target="tpu_custom_call" | custom-call | tf_op jit(solution)/shard_map/pallas_call | solution.py:370
  20.0 0.7 %shard_map.69 = (f32[64,512]{1,0:T(8,128)}, f32[1,128]{1,0:T(1,128)}) custom-call(f32[64,512]{1,0:T(8,128)S(1)} %get-tuple-element.6.x_ref, f32[8,128]{1,0:T(8,128)S(1)} %get-tuple-element.7.log_ref), custom_call_target="tpu_custom_call" | custom-call | tf_op jit(solution)/shard_map/pallas_call | solution.py:403

commit v4 on v3

--- a/solution.py
+++ b/solution.py
@@ -17,7 +17,11 @@
 MESH = pl.DeviceIdType.MESH
 UNROLL_LIMIT = 8
 EXTRA = 16
-ORDER = ((2, 3, 1), (0, 3, 2), (3, 0, 1), (2, 0, 1))
+ORDER = ((3, 2, 1), (0, 3, 2), (0, 3, 1), (0, 1, 2))
+WHOLE = tuple(order[-1] for order in ORDER)
+BELOW = ((), (0,), (0, 1), (0, 2, 1))
+ABOVE = ((2, 3, 1), (3, 2), (3,), ())
+FULL_PIECES = 2
 
 
 def dot(a, b):
@@ -74,7 +78,7 @@
         return lax.rem(chip + 1 + i, n_chip) * 2 + core
 
     def source(j):
-        if n_vec == 4:
+        if paired:
             first, *rest = (order[j] for order in ORDER)
             src = first
             for i, other in enumerate(rest):
@@ -146,19 +150,43 @@
         for k in range(pieces):
             along(dst, k).start()
 
-    if n_vec == 4:
-        pl.when(me == 3)(lambda: send_along(2))
-    each(others, lambda j: pl.when((j < me) & ((n_vec != 4) | (j != 2)))(lambda: send_along(j)))
-    load_own.start()
-    load_prop.start()
-
     def send_up(j):
         @pl.when(me + j + 1 < n_vec)
         def _():
             pl.semaphore_wait(z_ready.at[me + j], 1)
             send_along(me + j + 1)
 
-    send_up(0)
+    def core_rows(c, k):
+        part = rows // (2 * FULL_PIECES)
+        return pl.ds(pl.multiple_of((c * FULL_PIECES + k) * part, part), part)
+
+    def along_whole(src, dst, k):
+        return remote(chol_hbm.at[core_rows(core, k)], shared.at[src, core_rows(core, k)],
+                      v_send, z_recv.at[src - (src > dst), k], {"vec": dst})
+
+    def send(src, dst):
+        if dst > src:
+            pl.semaphore_wait(z_ready.at[dst - 1], 1)
+        if WHOLE[dst] == src:
+            for k in range(FULL_PIECES):
+                along_whole(src, dst, k).start()
+        else:
+            remote(chol_hbm.at[quarter(mw)], shared.at[src, quarter(mw)],
+                   v_send, z_recv.at[src - (src > dst), 0], {"vec": dst}).start()
+
+    def send_all(plan):
+        for v in range(n_vec):
+            @pl.when(me == v)
+            def _():
+                for d in plan[v]:
+                    send(v, d)
+
+    if paired:
+        send_all(BELOW)
+    else:
+        each(others, lambda j: pl.when(j < me)(lambda: send_along(j)))
+    load_own.start()
+    load_prop.start()
 
     load_orb.wait()
     pop[mw, 0:occ] = orb[...].astype(jnp.bfloat16)
@@ -174,9 +202,21 @@
 
     pl.when(core == 0)(lambda: pl.semaphore_wait(sib_ready, 1))
     walker(mw, 2 * chips, sibling).start()
-    each(chips, lambda j: pl.when(j + 1 > chip)(lambda: pl.semaphore_wait(x_ready.at[j], 1)))
-    for i in range(chips):
-        walker(mw, chips - 1 - i, peer(i)).start()
+    if paired:
+        pl.when(chip == 1)(lambda: walker(mw, 0, peer(0)).start())
+        send_all([d[:1] for d in ABOVE])
+
+        @pl.when(chip == 0)
+        def _():
+            pl.semaphore_wait(x_ready.at[0], 1)
+            walker(mw, 0, peer(0)).start()
+
+        send_all([d[1:] for d in ABOVE])
+    else:
+        each(chips, lambda j: pl.when(j + 1 > chip)(lambda: pl.semaphore_wait(x_ready.at[j], 1)))
+        for i in range(chips):
+            walker(mw, chips - 1 - i, peer(i)).start()
+        each(others, send_up)
 
     def take(j, k):
         src = source(j)
@@ -207,7 +247,7 @@
 
     def work(src, first, count):
         vectors = shared[src, pl.ds(pl.multiple_of(first * occ, occ), count * occ)]
-        s = dot(vectors, turned[...])
+        s = dot(vectors, turned[:, 0:occ])
         blocks = []
         for g in range(count):
             sg = s[g * occ:(g + 1) * occ, :]
@@ -215,7 +255,7 @@
             tg = jnp.sum(jnp.sum(on_diagonal, axis=0, keepdims=True), axis=1, keepdims=True)
             blocks.append((scale * (jnp.where(diagonal, tg, 0.0) - sg)).astype(jnp.bfloat16))
         adjoint = jnp.concatenate(blocks, axis=1) if count > 1 else blocks[0]
-        acc[...] += dot(adjoint, vectors)
+        acc[0:occ] += dot(adjoint, vectors)
 
     def pick(w):
         parent = jnp.broadcast_to(pop[w, occ:occ + 1, 3:4].astype(jnp.float32), (occ + EXTRA, basis))
@@ -270,26 +310,32 @@
         return remote(gsend, grecv, g_send, g_recv, {"wlk": peer(0)})
 
     if paired:
-        for j in range(1, others):
-            send_up(j)
         pass_walkers()
         turn_propagator()
         all_walkers()
         choose()
         load_own.wait()
         work_pair(me, False)
-        for j in range(others):
+        for j in range(others - 1):
             from_along(source(j), 0)
             beside(source(j), 0).start()
             if j > 0:
                 from_beside(source(j - 1))
                 work_pair(source(j - 1), False)
-        from_beside(source(others - 1))
-        work_pair(source(others - 1), True)
+        from_beside(source(others - 2))
+        work_pair(source(others - 2), True)
+        final = source(others - 1)
+        for k in range(FULL_PIECES):
+            view = shared.at[final, core_rows(core, k)]
+            remote(view, view, v_send, z_recv.at[slot(final, me), k], {"wlk": sibling}).wait_recv()
+            remote(view, view, v_send, near_recv.at[slot(final, me)], {"wlk": sibling}).start()
+        work(final, core * half, half)
+        view = shared.at[final, pl.ds(pl.multiple_of((1 - core) * (rows // 2), rows // 2), rows // 2)]
+        remote(view, view, v_send, near_recv.at[slot(final, me)], {"wlk": sibling}).wait_recv()
+        work(final, (1 - core) * half, half)
         give().wait_recv()
         acc[0:occ] += grecv[...].astype(jnp.float32)
     else:
-        each(others - 1, lambda j: send_up(j + 1))
         pass_walkers()
         turn_propagator()
         all_walkers()
@@ -329,8 +375,14 @@
     def sent(view, semaphore):
         remote(view, view, semaphore, semaphore, {"wlk": sibling}).wait_send()
 
+    def moved(v):
+        total = sum(rows // 2 if WHOLE[d] == v else share for d in range(n_vec) if d != v)
+        return (total + (others - 1) * share + rows // 2) // others
+
     if paired:
-        sent(shared.at[pl.ds(0, others), pl.ds(0, 2 * share)], v_send)
+        for v in range(n_vec):
+            view = shared.at[pl.ds(0, others), pl.ds(0, moved(v))]
+            pl.when(me == v)(functools.partial(sent, view, v_send))
         give().wait_send()
     else:
         sent(shared.at[pl.ds(0, others)], v_send)
@@ -357,7 +409,7 @@
         vecs = cholesky.shape[0]
         share = vecs * occ // n_wlk
         assert share * n_wlk == vecs * occ
-        paired = n_wlk == 4 and vecs % 2 == 0 and 2 <= n_vec <= UNROLL_LIMIT
+        paired = n_wlk == 4 and n_vec == 4 and vecs % 2 == 0
         pieces, walkers = 1, 2 if paired else 1
         others, chips = n_vec - 1, n_wlk // 2 - 1
         crossing = (1, 1) if paired else (others, chips)
@@ -383,7 +435,7 @@
                 pltpu.VMEM((occ, basis), bf16),
                 pltpu.VMEM((occ, basis), bf16),
                 dma((3,)),
-                dma((others, pieces)), dma(crossing + (pieces,)), dma((others,)), dma(crossing),
+                dma((others, FULL_PIECES)), dma(crossing + (pieces,)), dma((others,)), dma(crossing),
                 dma((2 * chips + 1,)), dma, dma, dma, dma,
                 regular((others,)), regular((chips,)), regular,
             ],

time: 21 us -> 20.6 us (0.981)
  the two profiles are of different devices: /device:TPU:25 before, /device:TPU:17 now
where the time goes in v4:
time: 20.6 us; the launch traced here: 20.4 us
  Pallas kernels  18.5 us (90%)
  between operations  1.93 us (9%)
    pallas_call x1, Pallas kernels, local(): pl.pallas_call(functools.partial(kernel, n_vec, n_wlk, vecs, pieces, pair...  17.8 us
    pallas_call x1, Pallas kernels, local(): pl.pallas_call(deliver, out_shape=(jax.ShapeDtypeStruct((occ, basis), f32...  0.68 us

profile of v4, /device:TPU:17, one launch (start us, length us, event | category | flops | bytes accessed | tf_op | source)
XLA Modules:
  0.0 20.4 jit_solution(9980285864746019688)
XLA Ops:
  1.9 17.8 %shard_map.68 = (f32[64,512]{1,0:T(8,128)S(1)}, f32[8,128]{1,0:T(8,128)S(1)}) custom-call(bf16[384,512]{1,0:T(8,128)(2,1)} %bitcast.5, f32[64,512]{1,0:T(8,128)} %bitcast.6, f32[1]{0:T(128)S(6)} %copy.7.logw, s32[1]{0:T(128)S(6)} %copy.8.par, f32[512,512]{1,0:T(8,128)} %prop_hbm.1), custom_call_target="tpu_custom_call" | custom-call | tf_op jit(solution)/shard_map/pallas_call | solution.py:422
  19.8 0.7 %shard_map.69 = (f32[64,512]{1,0:T(8,128)}, f32[1,128]{1,0:T(1,128)}) custom-call(f32[64,512]{1,0:T(8,128)S(1)} %get-tuple-element.6.x_ref, f32[8,128]{1,0:T(8,128)S(1)} %get-tuple-element.7.log_ref), custom_call_target="tpu_custom_call" | custom-call | tf_op jit(solution)/shard_map/pallas_call | solution.py:455

commit v5 on v4

--- a/solution.py
+++ b/solution.py
@@ -19,9 +19,12 @@
 EXTRA = 16
 ORDER = ((3, 2, 1), (0, 3, 2), (0, 3, 1), (0, 1, 2))
 WHOLE = tuple(order[-1] for order in ORDER)
-BELOW = ((), (0,), (0, 1), (0, 2, 1))
-ABOVE = ((2, 3, 1), (3, 2), (3,), ())
-FULL_PIECES = 2
+BELOW = ((), ((0,),), ((0,),), ((0,), (2,), (1,)))
+ABOVE = (((2,), (3,), (1,)), ((2, True, False), (3,)), ((3,),), ())
+LATE = ((), ((2, False, True),), ((1,),), ())
+FULL_PIECES = 3
+MIXED = (False, False, True, False)
+LEAN = 0
 
 
 def dot(a, b):
@@ -45,7 +48,7 @@
     chol_hbm, orb_hbm, logw, par, prop_hbm,
     out_ref, outlog_ref,
     orb, prop, propb, pop, turned, shared, acc, gsend, grecv,
-    load_sem, z_recv, x_recv, near_recv, far_recv, p_recv, g_recv, v_send, p_send, g_send,
+    load_sem, z_recv, x_recv, near_recv, far_recv, p_recv, g_recv, v_send, p_send, g_send, odd_send, last_recv,
     z_ready, x_ready, sib_ready,
 ):
     me = lax.axis_index("vec")
@@ -58,6 +61,7 @@
     chip, core = lax.div(mw, 2), lax.rem(mw, 2)
     sibling = mw + 1 - 2 * core
     others, chips = n_vec - 1, n_chip - 1
+    half = vecs // 2
     scale = 1.0 / math.sqrt(vecs * n_vec)
 
     def remote(src_ref, dst_ref, send, recv, where):
@@ -156,30 +160,54 @@
             pl.semaphore_wait(z_ready.at[me + j], 1)
             send_along(me + j + 1)
 
-    def core_rows(c, k):
-        part = rows // (2 * FULL_PIECES)
-        return pl.ds(pl.multiple_of((c * FULL_PIECES + k) * part, part), part)
-
-    def along_whole(src, dst, k):
-        return remote(chol_hbm.at[core_rows(core, k)], shared.at[src, core_rows(core, k)],
-                      v_send, z_recv.at[src - (src > dst), k], {"vec": dst})
-
-    def send(src, dst):
-        if dst > src:
+    batch = vecs // FULL_PIECES
+    alone = (FULL_PIECES - 1) * batch
+
+    def whole_parts(v):
+        parts = [(k * batch, batch) for k in range(FULL_PIECES)]
+        return parts[:-1] + [(alone + 1, batch - 1)] if MIXED[v] else parts
+
+    def core_rows(c, begin, count):
+        part = count * occ // 2
+        return pl.ds(pl.multiple_of(begin * occ + c * part, part), part)
+
+    def to_core(src, dst, begin, count, k):
+        remote(chol_hbm.at[core_rows(core, begin, count)], shared.at[src, core_rows(core, begin, count)],
+               v_send, z_recv.at[2 + k, 0], {"vec": dst}).start()
+
+    def halves(v, c):
+        if v == 0:
+            cut = min(half + LEAN, vecs - 1)
+            return (cut, vecs - cut) if c else (0, cut)
+        return c * half, half
+
+    def core_part(v, c, k):
+        begin, count = halves(v, c)
+        part = count * occ // 2
+        return pl.ds(pl.multiple_of(begin * occ + k * part, part), part)
+
+    def send_part(src, dst, c):
+        remote(chol_hbm.at[core_part(dst, c, core)], shared.at[src, core_part(dst, c, core)],
+               v_send if dst else odd_send, z_recv.at[ORDER[dst].index(src), 0], {"vec": dst}).start()
+
+    def send(src, dst, some=True, rest=True):
+        if dst > src and some:
             pl.semaphore_wait(z_ready.at[dst - 1], 1)
         if WHOLE[dst] == src:
-            for k in range(FULL_PIECES):
-                along_whole(src, dst, k).start()
+            if some and MIXED[dst]:
+                pl.when(chip == 0)(lambda: to_core(src, dst, alone, 1, FULL_PIECES))
+            for k, part in enumerate(whole_parts(dst) if rest else ()):
+                to_core(src, dst, *part, k)
         else:
-            remote(chol_hbm.at[quarter(mw)], shared.at[src, quarter(mw)],
-                   v_send, z_recv.at[src - (src > dst), 0], {"vec": dst}).start()
+            for c in range(2):
+                pl.when(chip == c)(functools.partial(send_part, src, dst, c))
 
     def send_all(plan):
         for v in range(n_vec):
             @pl.when(me == v)
             def _():
                 for d in plan[v]:
-                    send(v, d)
+                    send(v, *d)
 
     if paired:
         send_all(BELOW)
@@ -248,14 +276,15 @@
     def work(src, first, count):
         vectors = shared[src, pl.ds(pl.multiple_of(first * occ, occ), count * occ)]
         s = dot(vectors, turned[:, 0:occ])
-        blocks = []
+        swapped = (-scale * s).astype(jnp.bfloat16)
+        blocks = [swapped[g * occ:(g + 1) * occ, :] for g in range(count)]
+        direct = jnp.zeros((occ, basis), jnp.float32)
         for g in range(count):
-            sg = s[g * occ:(g + 1) * occ, :]
-            on_diagonal = jnp.where(diagonal, sg, 0.0)
+            on_diagonal = jnp.where(diagonal, s[g * occ:(g + 1) * occ, :], 0.0)
             tg = jnp.sum(jnp.sum(on_diagonal, axis=0, keepdims=True), axis=1, keepdims=True)
-            blocks.append((scale * (jnp.where(diagonal, tg, 0.0) - sg)).astype(jnp.bfloat16))
+            direct += (scale * tg) * vectors[g * occ:(g + 1) * occ].astype(jnp.float32)
         adjoint = jnp.concatenate(blocks, axis=1) if count > 1 else blocks[0]
-        acc[0:occ] += dot(adjoint, vectors)
+        acc[0:occ] += dot(adjoint, vectors) + direct
 
     def pick(w):
         parent = jnp.broadcast_to(pop[w, occ:occ + 1, 3:4].astype(jnp.float32), (occ + EXTRA, basis))
@@ -280,59 +309,89 @@
         load_prop.wait()
         propb[...] = prop[...].T.astype(jnp.bfloat16)
 
-    half = vecs // 2
     where = lax.broadcasted_iota(jnp.int32, (occ, 2 * occ), 1)
     left = where < occ
     pair_diagonal = lax.broadcasted_iota(jnp.int32, (occ, 2 * occ), 0) == jnp.where(
         left, where, where - occ)
 
-    def work_pair(src, last):
-        vectors = shared[src, pl.ds(pl.multiple_of(chip * half * occ, occ), half * occ)]
+    def work_pair(src, begin, count, last):
+        vectors = shared[src, pl.ds(pl.multiple_of(begin * occ, occ), count * occ)]
         s = dot(vectors, turned[...])
-        blocks = []
-        for g in range(half):
+        swapped = (-scale * s).astype(jnp.bfloat16)
+        blocks = [swapped[g * occ:(g + 1) * occ, :] for g in range(count)]
+        direct = [jnp.zeros((occ, basis), jnp.float32)] * 2
+        for g in range(count):
             sg = s[g * occ:(g + 1) * occ, :]
             along_diagonal = jnp.sum(jnp.where(pair_diagonal, sg, 0.0), axis=0, keepdims=True)
-            mine = jnp.sum(jnp.where(left[0:1], along_diagonal, 0.0), axis=1, keepdims=True)
-            theirs = jnp.sum(jnp.where(left[0:1], 0.0, along_diagonal), axis=1, keepdims=True)
-            trace = jnp.where(left, mine, theirs)
-            blocks.append((scale * (jnp.where(pair_diagonal, trace, 0.0) - sg)).astype(jnp.bfloat16))
+            block = vectors[g * occ:(g + 1) * occ].astype(jnp.float32)
+            for i in range(2):
+                side = jnp.where(left[0:1] if i == 0 else jnp.logical_not(left[0:1]), along_diagonal, 0.0)
+                direct[i] = direct[i] + scale * jnp.sum(side, axis=1, keepdims=True) * block
         mine = jnp.concatenate([b[:, 0:occ] for b in blocks], axis=1)
         theirs = jnp.concatenate([b[:, occ:] for b in blocks], axis=1)
         if last:
-            gsend[...] = (acc[occ:] + dot(theirs, vectors)).astype(jnp.bfloat16)
+            gsend[...] = (acc[occ:] + dot(theirs, vectors) + direct[1]).astype(jnp.bfloat16)
             give().start()
-            acc[0:occ] += dot(mine, vectors)
+            acc[0:occ] += dot(mine, vectors) + direct[0]
         else:
-            acc[...] += dot(jnp.concatenate([mine, theirs], axis=0), vectors)
+            acc[...] += dot(jnp.concatenate([mine, theirs], axis=0), vectors) + jnp.concatenate(
+                direct, axis=0)
+
+    def gather(v, c):
+        semaphore = v_send if v else odd_send
+        first, second, final = ORDER[v]
+
+        def landed(view, signal):
+            remote(view, view, v_send, signal, {"wlk": sibling}).wait_recv()
+
+        def pass_beside(view, send, signal):
+            remote(view, view, send, signal, {"wlk": sibling}).start()
+
+        def take(src):
+            view = shared.at[src, core_part(v, c, core)]
+            landed(view, z_recv.at[ORDER[v].index(src), 0])
+            pass_beside(view, semaphore, near_recv.at[src - (src > v)])
+
+        def finish(src, last):
+            landed(shared.at[src, core_part(v, c, 1 - core)], near_recv.at[src - (src > v)])
+            work_pair(src, *halves(v, c), last)
+
+        at_final = final - (final > v)
+        mixed = MIXED[v] and c == 0
+        take(first)
+        take(second)
+        finish(first, False)
+        finish(second, not mixed)
+        if mixed:
+            view = shared.at[final, core_rows(core, alone, 1)]
+            landed(view, z_recv.at[2 + FULL_PIECES, 0])
+            pass_beside(view, v_send, near_recv.at[at_final])
+            landed(shared.at[final, core_rows(1 - core, alone, 1)], near_recv.at[at_final])
+            work_pair(final, alone, 1, True)
+        parts = whole_parts(v)
+        for k in range(FULL_PIECES + 1):
+            if k < FULL_PIECES:
+                view = shared.at[final, core_rows(core, *parts[k])]
+                landed(view, z_recv.at[2 + k, 0])
+                pass_beside(view, v_send, last_recv.at[k])
+            if k > 0:
+                landed(shared.at[final, core_rows(1 - core, *parts[k - 1])], last_recv.at[k - 1])
+                work(final, *parts[k - 1])
 
     def give():
         return remote(gsend, grecv, g_send, g_recv, {"wlk": peer(0)})
 
     if paired:
         pass_walkers()
+        send_all(LATE)
         turn_propagator()
         all_walkers()
         choose()
         load_own.wait()
-        work_pair(me, False)
-        for j in range(others - 1):
-            from_along(source(j), 0)
-            beside(source(j), 0).start()
-            if j > 0:
-                from_beside(source(j - 1))
-                work_pair(source(j - 1), False)
-        from_beside(source(others - 2))
-        work_pair(source(others - 2), True)
-        final = source(others - 1)
-        for k in range(FULL_PIECES):
-            view = shared.at[final, core_rows(core, k)]
-            remote(view, view, v_send, z_recv.at[slot(final, me), k], {"wlk": sibling}).wait_recv()
-            remote(view, view, v_send, near_recv.at[slot(final, me)], {"wlk": sibling}).start()
-        work(final, core * half, half)
-        view = shared.at[final, pl.ds(pl.multiple_of((1 - core) * (rows // 2), rows // 2), rows // 2)]
-        remote(view, view, v_send, near_recv.at[slot(final, me)], {"wlk": sibling}).wait_recv()
-        work(final, (1 - core) * half, half)
+        work_pair(me, chip * half, half, False)
+        for v in range(n_vec):
+            for c in range(2):
+                pl.when((me == v) & (chip == c))(functools.partial(gather, v, c))
         give().wait_recv()
         acc[0:occ] += grecv[...].astype(jnp.float32)
     else:
@@ -375,14 +434,25 @@
     def sent(view, semaphore):
         remote(view, view, semaphore, semaphore, {"wlk": sibling}).wait_send()
 
-    def moved(v):
-        total = sum(rows // 2 if WHOLE[d] == v else share for d in range(n_vec) if d != v)
-        return (total + (others - 1) * share + rows // 2) // others
+    def whole_rows(v, c):
+        return (rows - (occ if MIXED[v] and c else 0)) // 2
+
+    def moved(v, c):
+        total = sum(whole_rows(d, c) if WHOLE[d] == v else share for d in range(1, n_vec) if d != v)
+        total += (whole_rows(0, c) if WHOLE[0] == v else 0) + whole_rows(v, c) + (2 * share if v else 0)
+        blocks = next(n for n in range(1, n_vec + 1) if total % n == 0 and total // n <= rows)
+        return shared.at[pl.ds(0, blocks), pl.ds(0, total // blocks)]
+
+    def odd_moved(v, c):
+        times = 2 if v == 0 else 0 if WHOLE[0] == v else 1
+        return times and shared.at[0, pl.ds(0, times * halves(0, c)[1] * occ // 2)]
 
     if paired:
         for v in range(n_vec):
-            view = shared.at[pl.ds(0, others), pl.ds(0, moved(v))]
-            pl.when(me == v)(functools.partial(sent, view, v_send))
+            for c in range(2):
+                pl.when((me == v) & (chip == c))(functools.partial(sent, moved(v, c), v_send))
+                if odd_moved(v, c):
+                    pl.when((me == v) & (chip == c))(functools.partial(sent, odd_moved(v, c), odd_send))
         give().wait_send()
     else:
         sent(shared.at[pl.ds(0, others)], v_send)
@@ -409,7 +479,7 @@
         vecs = cholesky.shape[0]
         share = vecs * occ // n_wlk
         assert share * n_wlk == vecs * occ
-        paired = n_wlk == 4 and n_vec == 4 and vecs % 2 == 0
+        paired = n_wlk == 4 and n_vec == 4 and vecs % (2 * FULL_PIECES) == 0
         pieces, walkers = 1, 2 if paired else 1
         others, chips = n_vec - 1, n_wlk // 2 - 1
         crossing = (1, 1) if paired else (others, chips)
@@ -435,8 +505,8 @@
                 pltpu.VMEM((occ, basis), bf16),
                 pltpu.VMEM((occ, basis), bf16),
                 dma((3,)),
-                dma((others, FULL_PIECES)), dma(crossing + (pieces,)), dma((others,)), dma(crossing),
-                dma((2 * chips + 1,)), dma, dma, dma, dma,
+                dma((FULL_PIECES + 3, 1) if paired else (others, pieces)), dma(crossing + (pieces,)), dma((others,)), dma(crossing),
+                dma((2 * chips + 1,)), dma, dma, dma, dma, dma, dma((FULL_PIECES,)),
                 regular((others,)), regular((chips,)), regular,
             ],
             compiler_params=pltpu.CompilerParams(

time: 20.6 us -> 20 us (0.971)
  the two profiles are of different devices: /device:TPU:17 before, /device:TPU:25 now
where the time goes in v5:
time: 20 us; the launch traced here: 19.9 us
  Pallas kernels  18 us (90%)
  between operations  1.93 us (10%)
    pallas_call x1, Pallas kernels, local(): pl.pallas_call(functools.partial(kernel, n_vec, n_wlk, vecs, pieces, pair...  17.3 us
    pallas_call x1, Pallas kernels, local(): pl.pallas_call(deliver, out_shape=(jax.ShapeDtypeStruct((occ, basis), f32...  0.68 us

profile of v5, /device:TPU:25, one launch (start us, length us, event | category | flops | bytes accessed | tf_op | source)
XLA Modules:
  0.0 19.9 jit_solution(233971764907729627)
XLA Ops:
  1.9 17.3 %shard_map.68 = (f32[64,512]{1,0:T(8,128)S(1)}, f32[8,128]{1,0:T(8,128)S(1)}) custom-call(bf16[384,512]{1,0:T(8,128)(2,1)} %bitcast.5, f32[64,512]{1,0:T(8,128)} %bitcast.6, f32[1]{0:T(128)S(6)} %copy.7.logw, s32[1]{0:T(128)S(6)} %copy.8.par, f32[512,512]{1,0:T(8,128)} %prop_hbm.1), custom_call_target="tpu_custom_call" | custom-call | tf_op jit(solution)/shard_map/pallas_call | solution.py:492
  19.2 0.7 %shard_map.69 = (f32[64,512]{1,0:T(8,128)}, f32[1,128]{1,0:T(1,128)}) custom-call(f32[64,512]{1,0:T(8,128)S(1)} %get-tuple-element.6.x_ref, f32[8,128]{1,0:T(8,128)S(1)} %get-tuple-element.7.log_ref), custom_call_target="tpu_custom_call" | custom-call | tf_op jit(solution)/shard_map/pallas_call | solution.py:525

commit v6 on v5

--- a/solution.py
+++ b/solution.py
@@ -24,7 +24,6 @@
 LATE = ((), ((2, False, True),), ((1,),), ())
 FULL_PIECES = 3
 MIXED = (False, False, True, False)
-LEAN = 0
 
 
 def dot(a, b):
@@ -48,7 +47,7 @@
     chol_hbm, orb_hbm, logw, par, prop_hbm,
     out_ref, outlog_ref,
     orb, prop, propb, pop, turned, shared, acc, gsend, grecv,
-    load_sem, z_recv, x_recv, near_recv, far_recv, p_recv, g_recv, v_send, p_send, g_send, odd_send, last_recv,
+    load_sem, z_recv, x_recv, near_recv, far_recv, p_recv, g_recv, v_send, p_send, g_send, last_recv,
     z_ready, x_ready, sib_ready,
 ):
     me = lax.axis_index("vec")
@@ -175,21 +174,6 @@
         remote(chol_hbm.at[core_rows(core, begin, count)], shared.at[src, core_rows(core, begin, count)],
                v_send, z_recv.at[2 + k, 0], {"vec": dst}).start()
 
-    def halves(v, c):
-        if v == 0:
-            cut = min(half + LEAN, vecs - 1)
-            return (cut, vecs - cut) if c else (0, cut)
-        return c * half, half
-
-    def core_part(v, c, k):
-        begin, count = halves(v, c)
-        part = count * occ // 2
-        return pl.ds(pl.multiple_of(begin * occ + k * part, part), part)
-
-    def send_part(src, dst, c):
-        remote(chol_hbm.at[core_part(dst, c, core)], shared.at[src, core_part(dst, c, core)],
-               v_send if dst else odd_send, z_recv.at[ORDER[dst].index(src), 0], {"vec": dst}).start()
-
     def send(src, dst, some=True, rest=True):
         if dst > src and some:
             pl.semaphore_wait(z_ready.at[dst - 1], 1)
@@ -199,8 +183,8 @@
             for k, part in enumerate(whole_parts(dst) if rest else ()):
                 to_core(src, dst, *part, k)
         else:
-            for c in range(2):
-                pl.when(chip == c)(functools.partial(send_part, src, dst, c))
+            remote(chol_hbm.at[quarter(mw)], shared.at[src, quarter(mw)],
+                   v_send, z_recv.at[ORDER[dst].index(src), 0], {"vec": dst}).start()
 
     def send_all(plan):
         for v in range(n_vec):
@@ -337,43 +321,48 @@
             acc[...] += dot(jnp.concatenate([mine, theirs], axis=0), vectors) + jnp.concatenate(
                 direct, axis=0)
 
-    def gather(v, c):
-        semaphore = v_send if v else odd_send
+    def gather(v):
         first, second, final = ORDER[v]
 
         def landed(view, signal):
             remote(view, view, v_send, signal, {"wlk": sibling}).wait_recv()
 
-        def pass_beside(view, send, signal):
-            remote(view, view, send, signal, {"wlk": sibling}).start()
+        def pass_beside(view, signal):
+            remote(view, view, v_send, signal, {"wlk": sibling}).start()
 
         def take(src):
-            view = shared.at[src, core_part(v, c, core)]
+            view = shared.at[src, quarter(mw)]
             landed(view, z_recv.at[ORDER[v].index(src), 0])
-            pass_beside(view, semaphore, near_recv.at[src - (src > v)])
+            pass_beside(view, near_recv.at[src - (src > v)])
 
         def finish(src, last):
-            landed(shared.at[src, core_part(v, c, 1 - core)], near_recv.at[src - (src > v)])
-            work_pair(src, *halves(v, c), last)
+            landed(shared.at[src, quarter(sibling)], near_recv.at[src - (src > v)])
+            work_pair(src, chip * half, half, last)
 
         at_final = final - (final > v)
-        mixed = MIXED[v] and c == 0
         take(first)
         take(second)
         finish(first, False)
-        finish(second, not mixed)
-        if mixed:
+
+        def lone():
+            finish(second, False)
             view = shared.at[final, core_rows(core, alone, 1)]
             landed(view, z_recv.at[2 + FULL_PIECES, 0])
-            pass_beside(view, v_send, near_recv.at[at_final])
+            pass_beside(view, near_recv.at[at_final])
             landed(shared.at[final, core_rows(1 - core, alone, 1)], near_recv.at[at_final])
             work_pair(final, alone, 1, True)
+
+        if MIXED[v]:
+            pl.when(chip == 0)(lone)
+            pl.when(chip == 1)(lambda: finish(second, True))
+        else:
+            finish(second, True)
         parts = whole_parts(v)
         for k in range(FULL_PIECES + 1):
             if k < FULL_PIECES:
                 view = shared.at[final, core_rows(core, *parts[k])]
                 landed(view, z_recv.at[2 + k, 0])
-                pass_beside(view, v_send, last_recv.at[k])
+                pass_beside(view, last_recv.at[k])
             if k > 0:
                 landed(shared.at[final, core_rows(1 - core, *parts[k - 1])], last_recv.at[k - 1])
                 work(final, *parts[k - 1])
@@ -390,8 +379,7 @@
         load_own.wait()
         work_pair(me, chip * half, half, False)
         for v in range(n_vec):
-            for c in range(2):
-                pl.when((me == v) & (chip == c))(functools.partial(gather, v, c))
+            pl.when(me == v)(functools.partial(gather, v))
         give().wait_recv()
         acc[0:occ] += grecv[...].astype(jnp.float32)
     else:
@@ -438,21 +426,15 @@
         return (rows - (occ if MIXED[v] and c else 0)) // 2
 
     def moved(v, c):
-        total = sum(whole_rows(d, c) if WHOLE[d] == v else share for d in range(1, n_vec) if d != v)
-        total += (whole_rows(0, c) if WHOLE[0] == v else 0) + whole_rows(v, c) + (2 * share if v else 0)
+        total = sum(whole_rows(d, c) if WHOLE[d] == v else share for d in range(n_vec) if d != v)
+        total += whole_rows(v, c) + 2 * share
         blocks = next(n for n in range(1, n_vec + 1) if total % n == 0 and total // n <= rows)
         return shared.at[pl.ds(0, blocks), pl.ds(0, total // blocks)]
-
-    def odd_moved(v, c):
-        times = 2 if v == 0 else 0 if WHOLE[0] == v else 1
-        return times and shared.at[0, pl.ds(0, times * halves(0, c)[1] * occ // 2)]
 
     if paired:
         for v in range(n_vec):
             for c in range(2):
                 pl.when((me == v) & (chip == c))(functools.partial(sent, moved(v, c), v_send))
-                if odd_moved(v, c):
-                    pl.when((me == v) & (chip == c))(functools.partial(sent, odd_moved(v, c), odd_send))
         give().wait_send()
     else:
         sent(shared.at[pl.ds(0, others)], v_send)
@@ -506,7 +488,7 @@
                 pltpu.VMEM((occ, basis), bf16),
                 dma((3,)),
                 dma((FULL_PIECES + 3, 1) if paired else (others, pieces)), dma(crossing + (pieces,)), dma((others,)), dma(crossing),
-                dma((2 * chips + 1,)), dma, dma, dma, dma, dma, dma((FULL_PIECES,)),
+                dma((2 * chips + 1,)), dma, dma, dma, dma, dma((FULL_PIECES,)),
                 regular((others,)), regular((chips,)), regular,
             ],
             compiler_params=pltpu.CompilerParams(

time: 20 us -> 20 us (level)
  no operation moved by 1% of the time
where the time goes in v6:
time: 20 us; the launch traced here: 19.9 us
  Pallas kernels  18 us (90%)
  between operations  1.93 us (10%)
    pallas_call x1, Pallas kernels, local(): pl.pallas_call(functools.partial(kernel, n_vec, n_wlk, vecs, pieces, pair...  17.3 us
    pallas_call x1, Pallas kernels, local(): pl.pallas_call(deliver, out_shape=(jax.ShapeDtypeStruct((occ, basis), f32...  0.68 us

profile of v6, /device:TPU:25, one launch (start us, length us, event | category | flops | bytes accessed | tf_op | source)
XLA Modules:
  0.0 19.9 jit_solution(11610618259941988644)
XLA Ops:
  1.9 17.3 %shard_map.68 = (f32[64,512]{1,0:T(8,128)S(1)}, f32[8,128]{1,0:T(8,128)S(1)}) custom-call(bf16[384,512]{1,0:T(8,128)(2,1)} %bitcast.5, f32[64,512]{1,0:T(8,128)} %bitcast.6, f32[1]{0:T(128)S(6)} %copy.7.logw, s32[1]{0:T(128)S(6)} %copy.8.par, f32[512,512]{1,0:T(8,128)} %prop_hbm.1), custom_call_target="tpu_custom_call" | custom-call | tf_op jit(solution)/shard_map/pallas_call | solution.py:474
  19.2 0.7 %shard_map.69 = (f32[64,512]{1,0:T(8,128)}, f32[1,128]{1,0:T(1,128)}) custom-call(f32[64,512]{1,0:T(8,128)S(1)} %get-tuple-element.6.x_ref, f32[8,128]{1,0:T(8,128)S(1)} %get-tuple-element.7.log_ref), custom_call_target="tpu_custom_call" | custom-call | tf_op jit(solution)/shard_map/pallas_call | solution.py:507

commit v7 on v6

--- a/solution.py
+++ b/solution.py
@@ -144,11 +144,6 @@
     before = me + chip + core
     pl.when(before > 0)(lambda: pl.semaphore_wait(barrier, before))
 
-    each(others, lambda j: pl.when(j < me)(lambda: greet(z_ready.at[me - 1], {"vec": j})))
-    each(chips, lambda j: pl.when(j < chip)(
-        lambda: greet(x_ready.at[chip - 1], {"wlk": j * 2 + core})))
-    pl.when(core == 1)(lambda: greet(sib_ready, {"wlk": sibling}))
-
     def send_along(dst):
         for k in range(pieces):
             along(dst, k).start()
@@ -197,6 +192,11 @@
         send_all(BELOW)
     else:
         each(others, lambda j: pl.when(j < me)(lambda: send_along(j)))
+    each(others, lambda j: pl.when(j < me)(lambda: greet(z_ready.at[me - 1], {"vec": j})))
+    each(chips, lambda j: pl.when(j < chip)(
+        lambda: greet(x_ready.at[chip - 1], {"wlk": j * 2 + core})))
+    pl.when(core == 1)(lambda: greet(sib_ready, {"wlk": sibling}))
+
     load_own.start()
     load_prop.start()
 

time: 20 us -> 20 us (level)
  no operation moved by 1% of the time
where the time goes in v7:
time: 20 us; the launch traced here: 19.9 us
  Pallas kernels  18 us (90%)
  between operations  1.93 us (10%)
    pallas_call x1, Pallas kernels, local(): pl.pallas_call(functools.partial(kernel, n_vec, n_wlk, vecs, pieces, pair...  17.3 us
    pallas_call x1, Pallas kernels, local(): pl.pallas_call(deliver, out_shape=(jax.ShapeDtypeStruct((occ, basis), f32...  0.68 us

profile of v7, /device:TPU:25, one launch (start us, length us, event | category | flops | bytes accessed | tf_op | source)
XLA Modules:
  0.0 19.9 jit_solution(15587049504077341884)
XLA Ops:
  1.9 17.3 %shard_map.68 = (f32[64,512]{1,0:T(8,128)S(1)}, f32[8,128]{1,0:T(8,128)S(1)}) custom-call(bf16[384,512]{1,0:T(8,128)(2,1)} %bitcast.5, f32[64,512]{1,0:T(8,128)} %bitcast.6, f32[1]{0:T(128)S(6)} %copy.7.logw, s32[1]{0:T(128)S(6)} %copy.8.par, f32[512,512]{1,0:T(8,128)} %prop_hbm.1), custom_call_target="tpu_custom_call" | custom-call | tf_op jit(solution)/shard_map/pallas_call | solution.py:474
  19.2 0.7 %shard_map.69 = (f32[64,512]{1,0:T(8,128)}, f32[1,128]{1,0:T(1,128)}) custom-call(f32[64,512]{1,0:T(8,128)S(1)} %get-tuple-element.6.x_ref, f32[8,128]{1,0:T(8,128)S(1)} %get-tuple-element.7.log_ref), custom_call_target="tpu_custom_call" | custom-call | tf_op jit(solution)/shard_map/pallas_call | solution.py:507
